TPU v7x, 256 devices: a whole 4x4x8 slice. The times are simulated.
256 devices in a mesh: level: 4 (over z_lo, core), tile: 64 (over x, z_hi, y).
Axes of the slice: x: 4, y: 4, z: 8 (z_hi: 4, z_lo: 2; z = z_hi * 2 + z_lo), core: 2. Of those that a mesh axis runs over, the one named last changes fastest.
Arguments:
- queue_init: bfloat16 [4, 4, 4, 256, 128], P('level', None, None, 'tile'), may hold values from -6 to 6
- noise_frames: bfloat16 [2, 4, 4, 256, 128], P(None, None, None, 'tile'), may hold values from -6 to 6
- conv_first: bfloat16 [3, 3, 320, 4], replicated, may hold values from -1 to 1
- conv_second: bfloat16 [3, 3, 320, 320], replicated, may hold values from -0.109375 to 0.109375
- time_weight: bfloat16 [3, 320, 320], replicated, may hold values from -0.1875 to 0.1875
- out_proj: bfloat16 [4, 320], replicated, may hold values from -0.3125 to 0.3125
- keep_coef: float32 [2, 4, 4], replicated, may hold values from 0.6 to 1
- noise_coef: float32 [2, 4, 4], replicated, may hold values from 0.1 to 0.5
Outputs:
- queue_final: bfloat16 [4, 4, 4, 256, 128], P('level', None, None, 'tile')
All inputs are finite; a program needn't handle non-finite values.
Results may differ from a plain program's by a relative error of at most 0.0048.
Values may be sent and summed in bfloat16 or wider, within the bound.
A program may use at most 64 MiB of HBM per device.

v0:
```python
import jax
import jax.numpy as jnp
from jax import lax
from jax.sharding import PartitionSpec as P

STEPS = 2


def with_halo(block, sides, width):
    for axis, dim in sides:
        count = lax.axis_size(axis)
        forward = [(i, i + 1) for i in range(count - 1)]
        backward = [(target, source) for source, target in forward]
        low = lax.ppermute(
            lax.slice_in_dim(block, block.shape[dim] - width, None, axis=dim), axis, forward
        )
        high = lax.ppermute(lax.slice_in_dim(block, 0, width, axis=dim), axis, backward)
        block = jnp.concatenate([low, block, high], axis=dim)
    return block


def shifted(value, axis, steps):
    count = lax.axis_size(axis)
    leading, last = (max(0, -steps), min(count, count - steps))
    return lax.ppermute(value, axis, [(source, source + steps) for source in range(leading, last)])


def conv_rows(extended, weight, row_count):
    padded = jnp.pad(extended, ((0, 0), (0, 0), (0, 0), (1, 1)))
    col_count = extended.shape[3]
    running = jnp.zeros((extended.shape[0], weight.shape[2], row_count, col_count), jnp.float32)
    for row_tap in range(3):
        for col_tap in range(3):
            window = padded[:, :, row_tap : row_tap + row_count, col_tap : col_tap + col_count]
            running = running + jnp.einsum(
                "oc,fchw->fohw",
                weight[row_tap, col_tap],
                window,
                preferred_element_type=jnp.float32,
            )
    return running


def time_terms(active, time_weight):
    extended = with_halo(active, (("level", 0),), 1)
    frame_count = active.shape[0]
    running = jnp.einsum(
        "oc,fchw->fohw", time_weight[0], extended[0:frame_count], preferred_element_type=jnp.float32
    )
    running = running + jnp.einsum(
        "oc,fchw->fohw",
        time_weight[1],
        extended[1 : frame_count + 1],
        preferred_element_type=jnp.float32,
    )
    running = running + jnp.einsum(
        "oc,fchw->fohw",
        time_weight[2],
        extended[2 : frame_count + 2],
        preferred_element_type=jnp.float32,
    )
    return running


def per_device(
    queue_init, noise_frames, conv_first, conv_second, time_weight, out_proj, keep_coef, noise_coef
):
    queued = queue_init[0]
    row_count = queued.shape[2]
    position = lax.axis_index("level")
    for step_index in range(STEPS):
        queued = shifted(queued, "level", 1)
        queued = jnp.where(position == 0, noise_frames[step_index], queued)
        extended = with_halo(queued, (("tile", 2),), 2)
        first_act = jax.nn.silu(conv_rows(extended, conv_first, row_count + 2))
        global_rows = (
            lax.axis_index("tile") * row_count + jnp.arange(row_count + 2, dtype=jnp.int32) - 1
        )
        inside = (global_rows >= 0) & (global_rows < row_count * lax.axis_size("tile"))
        first_act = jnp.where(inside[None, None, :, None], first_act, 0.0).astype(jnp.bfloat16)
        second = conv_rows(first_act, conv_second, row_count)
        active = jax.nn.silu(second).astype(jnp.bfloat16)
        predicted = (second + time_terms(active, time_weight)).astype(jnp.bfloat16)
        projected = jnp.einsum(
            "oc,fchw->fohw", out_proj, predicted, preferred_element_type=jnp.float32
        )
        keep_rate = lax.dynamic_index_in_dim(keep_coef[step_index], position, 0, keepdims=False)
        noise_rate = lax.dynamic_index_in_dim(noise_coef[step_index], position, 0, keepdims=False)
        queued = (
            keep_rate[:, None, None, None] * queued.astype(jnp.float32)
            - noise_rate[:, None, None, None] * projected
        ).astype(jnp.bfloat16)
    return queued[None]


def solution(mesh):
    return jax.shard_map(
        per_device,
        mesh=mesh,
        in_specs=(
            P("level", None, None, "tile", None),
            P(None, None, None, "tile", None),
            P(),
            P(),
            P(),
            P(),
            P(),
            P(),
        ),
        out_specs=P("level", None, None, "tile", None),
        check_vma=False,
    )
```

profile of v0, /device:TPU:7, one launch (start us, length us, event | category | flops | bytes accessed | tf_op | source)
XLA Modules:
  0.0 135.9 jit_solution(5128710707599088948)
XLA Ops:
  0.0 0.7 copy.44
  0.8 4.1 %collective-permute-start = (bf16[4,4,4,128]{3,1,2,0:T(4,128)(2,1)S(1)}, bf16[4,4,4,128]{3,1,2,0:T(4,128)(2,1)S(1)}, u32[]{:S(2)}, u32[]{:S(2)}) collective-permute-start(bf16[4,4,4,128]{3,1,2,0:T(4,128)(2,1)S(1)} %bitcast.335), channel_id=1, source_target_pairs={{0,64},{64,128},{128,192},{1,65},{65,129},{129,193},{2,66},{66,130... | collective-permute-start | bytes 49160 | tf_op jit(solution)/shard_map/ppermute | solution.py:25
  4.9 1.4 fusion.225
  6.2 0.7 fusion.228
  6.9 0.7 fusion.229
  7.6 0.5 fusion.186
  8.2 3.2 %collective-permute-start.1 = (bf16[4,4,2,128]{3,1,2,0:T(4,128)(2,1)S(1)}, bf16[4,4,2,128]{3,1,2,0:T(4,128)(2,1)S(1)}, u32[]{:S(2)}, u32[]{:S(2)}) collective-permute-start(bf16[4,4,2,128]{3,1,2,0:T(4,128)(2,1)S(1)} %get-tuple-element.13), channel_id=1, source_target_pairs={{0,1},{1,2},{2,3},{3,4},{4,5},{5,6},{6,7},{7,8},{8,9},{9,10},{10,1... | collective-permute-start | bytes 24584 | tf_op jit(solution)/shard_map/ppermute | solution.py:14
  11.4 8.5 %collective-permute-start.2 = (bf16[4,4,2,128]{3,1,2,0:T(4,128)(2,1)S(1)}, bf16[4,4,2,128]{3,1,2,0:T(4,128)(2,1)S(1)}, u32[]{:S(2)}, u32[]{:S(2)}) collective-permute-start(bf16[4,4,2,128]{3,1,2,0:T(4,128)(2,1)S(1)} %get-tuple-element.14), channel_id=1, source_target_pairs={{1,0},{2,1},{3,2},{4,3},{5,4},{6,5},{7,6},{8,7},{9,8},{10,9},{11,1... | collective-permute-start | bytes 24584 | tf_op jit(solution)/shard_map/ppermute | solution.py:17
  19.9 0.7 collective-permute-done.2
  20.7 1.4 %fusion.110 = f32[4,6,128,320]{2,3,1,0:T(8,128)S(1)} fusion(bf16[4,4,8,128]{3,1,2,0:T(4,128)(2,1)S(1)} %pad_maximum_fusion.24, bf16[3,3,320,4]{2,3,1,0:T(4,128)(2,1)} %param.10), kind=kOutput, calls=%fused_computation.150 | convolution fusion | flops 7864320 | bytes 3968000 | tf_op jit(solution)/shard_map/oc,fchw->fohw/dot_general | solution.py:35
  22.1 0.7 fusion.111
  22.8 0.7 fusion.112
  23.6 0.7 fusion.113
  24.3 2.6 %fusion.114 = f32[4,6,128,320]{2,3,1,0:T(8,128)} fusion(bf16[4,4,8,128]{3,1,2,0:T(4,128)(2,1)S(1)} %pad_maximum_fusion.24, bf16[3,3,320,4]{2,3,1,0:T(4,128)(2,1)S(1)} %copy-done.5), kind=kOutput, calls=%fused_computation.154 | convolution fusion | flops 7864320 | bytes 3968000 | tf_op jit(solution)/shard_map/oc,fchw->fohw/dot_general | solution.py:35
  26.9 2.6 %fusion.157 = f32[4,6,128,320]{2,3,1,0:T(8,128)} fusion(bf16[3,3,320,4]{2,3,1,0:T(4,128)(2,1)S(1)} %copy-done.5, bf16[4,4,2,128]{3,1,2,0:T(4,128)(2,1)S(1)} %collective-permute-done.2, bf16[4,4,4,128]{3,1,2,0:T(4,128)(2,1)S(1)} %fusion.139, bf16[4,4,2,128]{3,1,2,0:T(4,128)(2,1)S(1)} %collective-permute-done.1), kind=kOutput, calls=%fused_computation.196 | convolution fusion | flops 7962624 | bytes 3968000 | tf_op jit(solution)/shard_map/oc,fchw->fohw/dot_general | solution.py:35
  29.5 2.6 %fusion.122 = f32[4,6,128,320]{2,3,1,0:T(8,128)} fusion(bf16[4,4,4,128]{3,1,2,0:T(4,128)(2,1)S(1)} %fusion.139, bf16[4,4,2,128]{3,1,2,0:T(4,128)(2,1)S(1)} %collective-permute-done.1, bf16[3,3,320,4]{2,3,1,0:T(4,128)(2,1)S(1)} %copy-done.5), kind=kOutput, calls=%fused_computation.162 | convolution fusion | flops 7913472 | bytes 3959808 | tf_op jit(solution)/shard_map/oc,fchw->fohw/dot_general | solution.py:35
  32.1 2.6 %fusion.126 = f32[4,6,128,320]{2,3,1,0:T(8,128)} fusion(bf16[4,4,2,128]{3,1,2,0:T(4,128)(2,1)S(1)} %collective-permute-done.2, bf16[4,4,4,128]{3,1,2,0:T(4,128)(2,1)S(1)} %fusion.139, bf16[3,3,320,4]{2,3,1,0:T(4,128)(2,1)S(1)} %copy-done.5), kind=kOutput, calls=%fused_computation.166 | convolution fusion | flops 7913472 | bytes 3959808 | tf_op jit(solution)/shard_map/oc,fchw->fohw/dot_general | solution.py:35
  34.7 6.9 %fusion.8 = bf16[4,320,6,128]{3,1,2,0:T(8,128)(2,1)S(1)} fusion(f32[4,6,128,320]{2,3,1,0:T(8,128)} %fusion.126, f32[4,6,128,320]{2,3,1,0:T(8,128)} %fusion.114, f32[4,6,128,320]{2,3,1,0:T(8,128)S(1)} %fusion.113, f32[4,6,128,320]{2,3,1,0:T(8,128)} %fusion.157, f32[4,6,128,320]{2,3,1,0:T(8,128)S(1)} %fusion.112, f32[4,6,128,320]{2,3,1,0:T(8,128)S(1)} %fusion.111, ...), kind=kOutput, calls=%fused_computation.24 | convolution fusion | flops 21626880 | bytes 33459712 | tf_op jit(solution)/shard_map/oc,fchw->fohw/dot_general | solution.py:35
  41.7 2.0 %fusion.20 = f32[4,4,128,320]{2,3,1,0:T(8,128)S(1)} fusion(bf16[4,320,6,128]{3,1,2,0:T(8,128)(2,1)S(1)} %fusion.8, bf16[3,3,320,320]{3,2,1,0:T(8,128)(2,1)} %param.11), kind=kOutput, calls=%fused_computation.44 | convolution fusion | flops 419430400 | bytes 4833280 | tf_op jit(solution)/shard_map/oc,fchw->fohw/dot_general | solution.py:35
  43.7 0.9 fusion.21
  44.7 1.0 fusion.22
  45.6 0.9 fusion.23
  46.6 1.0 fusion.24
  47.6 0.8 fusion.44
  48.4 0.8 fusion.46
  49.2 0.8 fusion.48
  50.1 3.8 %fusion.18 = (bf16[4,320,4,128]{3,1,2,0:T(8,128)(2,1)S(1)}, f32[4,4,128,320]{2,3,1,0:T(8,128)}) fusion(bf16[4,320,6,128]{3,1,2,0:T(8,128)(2,1)S(1)} %fusion.8, bf16[3,3,320,320]{3,2,1,0:T(8,128)(2,1)S(1)} %copy-done.1, f32[4,4,128,320]{2,3,1,0:T(8,128)S(1)} %fusion.44, f32[4,4,128,320]{2,3,1,0:T(8,128)S(1)} %fusion.24, f32[4,4,128,320]{2,3,1,0:T(8,128)S(1)} %fusion.23, ...), kind=kOutput, calls=%fused_computation.42 | convolution fusion | flops 427950080 | bytes 27115520 | tf_op jit(solution)/shard_map/oc,fchw->fohw/dot_general | solution.py:35
  54.0 2.8 %collective-permute-start.3 = (bf16[1,320,4,128]{3,1,2,0:T(8,128)(2,1)S(1)}, bf16[1,320,4,128]{3,1,2,0:T(8,128)(2,1)S(1)}, u32[]{:S(2)}, u32[]{:S(2)}) collective-permute-start(bf16[1,320,4,128]{3,1,2,0:T(8,128)(2,1)S(1)} %get-tuple-element.8), channel_id=1, source_target_pairs={{0,64},{64,128},{128,192},{1,65},{65,129},{129,193},{2,66},{66,130... | collective-permute-start | bytes 983048 | tf_op jit(solution)/shard_map/ppermute | solution.py:14
  56.8 1.9 %collective-permute-start.4 = (bf16[1,320,4,128]{3,1,2,0:T(8,128)(2,1)S(1)}, bf16[1,320,4,128]{3,1,2,0:T(8,128)(2,1)S(1)}, u32[]{:S(2)}, u32[]{:S(2)}) collective-permute-start(bf16[1,320,4,128]{3,1,2,0:T(8,128)(2,1)S(1)} %get-tuple-element.7), channel_id=1, source_target_pairs={{64,0},{128,64},{192,128},{65,1},{129,65},{193,129},{66,2},{130,66... | collective-permute-start | bytes 983048 | tf_op jit(solution)/shard_map/ppermute | solution.py:17
  58.7 2.3 %fusion.60 = f32[4,4,128,320]{2,3,1,0:T(8,128)} fusion(bf16[4,320,4,128]{3,1,2,0:T(8,128)(2,1)S(1)} %get-tuple-element.19, bf16[3,320,320]{2,1,0:T(8,128)(2,1)S(1)} %copy-done.3), kind=kOutput, calls=%fused_computation.86 | convolution fusion | flops 419430400 | bytes 4177920 | tf_op jit(solution)/shard_map/oc,fchw->fohw/dot_general | solution.py:50
  61.0 2.4 %fusion.42 = f32[4,4,128,320]{2,3,1,0:T(8,128)} fusion(bf16[4,320,4,128]{3,1,2,0:T(8,128)(2,1)S(1)} %get-tuple-element.19, bf16[1,320,4,128]{3,1,2,0:T(8,128)(2,1)S(1)} %collective-permute-done.3, bf16[3,320,320]{2,1,0:T(8,128)(2,1)S(1)} %copy-done.3), kind=kOutput, calls=%fused_computation.70 | convolution fusion | flops 422051840 | bytes 4505600 | tf_op jit(solution)/shard_map/oc,fchw->fohw/dot_general | solution.py:47
  63.4 1.7 %collective-permute-done.4 = bf16[1,320,4,128]{3,1,2,0:T(8,128)(2,1)S(1)} collective-permute-done((bf16[1,320,4,128]{3,1,2,0:T(8,128)(2,1)S(1)}, bf16[1,320,4,128]{3,1,2,0:T(8,128)(2,1)S(1)}, u32[]{:S(2)}, u32[]{:S(2)}) %collective-permute-start.4) | collective-permute-done | bytes 327712 | tf_op jit(solution)/shard_map/ppermute | solution.py:17
  65.2 4.5 %subtract_convert_fusion.1 = bf16[4,4,4,128]{3,1,2,0:T(4,128)(2,1)S(1)} fusion(bf16[4,4,4,128]{3,1,2,0:T(4,128)(2,1)S(1)} %fusion.139, f32[4,4,128,320]{2,3,1,0:T(8,128)} %get-tuple-element.20, f32[4,4,128,320]{2,3,1,0:T(8,128)} %fusion.42, f32[4,4,128,320]{2,3,1,0:T(8,128)} %fusion.60, bf16[1,320,4,128]{3,1,2,0:T(8,128)(2,1)S(1)} %collective-permute-done.4, ...), kind=kOutput, calls=%fused_computation.149 | convolution fusion | flops 429957120 | bytes 9783840 | tf_op jit(solution)/shard_map/oc,fchw->fohw/dot_general | solution.py:84
  69.7 2.4 %collective-permute-start.5 = (bf16[4,4,4,128]{3,1,2,0:T(4,128)(2,1)S(1)}, bf16[4,4,4,128]{3,1,2,0:T(4,128)(2,1)S(1)}, u32[]{:S(2)}, u32[]{:S(2)}) collective-permute-start(bf16[4,4,4,128]{3,1,2,0:T(4,128)(2,1)S(1)} %subtract_convert_fusion.1), channel_id=1, source_target_pairs={{0,64},{64,128},{128,192},{1,65},{65,129},{129,193},{2,66},{66,130... | collective-permute-start | bytes 49160 | tf_op jit(solution)/shard_map/ppermute | solution.py:25
  72.1 0.8 collective-permute-done.5
  73.0 1.9 %collective-permute-start.6 = (bf16[4,4,2,128]{3,1,2,0:T(4,128)(2,1)S(1)}, bf16[4,4,2,128]{3,1,2,0:T(4,128)(2,1)S(1)}, u32[]{:S(2)}, u32[]{:S(2)}) collective-permute-start(bf16[4,4,2,128]{3,1,2,0:T(4,128)(2,1)S(1)} %get-tuple-element.11), channel_id=1, source_target_pairs={{0,1},{1,2},{2,3},{3,4},{4,5},{5,6},{6,7},{7,8},{8,9},{9,10},{10,1... | collective-permute-start | bytes 24584 | tf_op jit(solution)/shard_map/ppermute | solution.py:14
  74.9 9.2 %collective-permute-start.7 = (bf16[4,4,2,128]{3,1,2,0:T(4,128)(2,1)S(1)}, bf16[4,4,2,128]{3,1,2,0:T(4,128)(2,1)S(1)}, u32[]{:S(2)}, u32[]{:S(2)}) collective-permute-start(bf16[4,4,2,128]{3,1,2,0:T(4,128)(2,1)S(1)} %get-tuple-element.12), channel_id=1, source_target_pairs={{1,0},{2,1},{3,2},{4,3},{5,4},{6,5},{7,6},{8,7},{9,8},{10,9},{11,1... | collective-permute-start | bytes 24584 | tf_op jit(solution)/shard_map/ppermute | solution.py:17
  84.2 0.5 fusion.185
  84.7 0.0 collective-permute-done.7
  84.8 0.7 fusion.116
  85.5 0.7 fusion.117
  86.2 0.7 fusion.118
  86.9 0.7 fusion.119
  87.7 2.6 %fusion.120 = f32[4,6,128,320]{2,3,1,0:T(8,128)} fusion(bf16[4,4,8,128]{3,1,2,0:T(4,128)(2,1)S(1)} %pad_maximum_fusion.25, bf16[3,3,320,4]{2,3,1,0:T(4,128)(2,1)S(1)} %copy-done.6), kind=kOutput, calls=%fused_computation.160 | convolution fusion | flops 7864320 | bytes 3968000 | tf_op jit(solution)/shard_map/oc,fchw->fohw/dot_general | solution.py:35
  90.3 2.6 %fusion.130 = f32[4,6,128,320]{2,3,1,0:T(8,128)} fusion(bf16[4,4,4,128]{3,1,2,0:T(4,128)(2,1)S(1)} %fusion.140, bf16[4,4,2,128]{3,1,2,0:T(4,128)(2,1)S(1)} %collective-permute-done.6, bf16[3,3,320,4]{2,3,1,0:T(4,128)(2,1)S(1)} %copy-done.6), kind=kOutput, calls=%fused_computation.170 | convolution fusion | flops 7913472 | bytes 3959808 | tf_op jit(solution)/shard_map/oc,fchw->fohw/dot_general | solution.py:35
  92.9 2.6 %fusion.155 = f32[4,6,128,320]{2,3,1,0:T(8,128)} fusion(bf16[3,3,320,4]{2,3,1,0:T(4,128)(2,1)S(1)} %copy-done.6, bf16[4,4,2,128]{3,1,2,0:T(4,128)(2,1)S(1)} %collective-permute-done.7, bf16[4,4,4,128]{3,1,2,0:T(4,128)(2,1)S(1)} %fusion.140, bf16[4,4,2,128]{3,1,2,0:T(4,128)(2,1)S(1)} %collective-permute-done.6), kind=kOutput, calls=%fused_computation.194 | convolution fusion | flops 7962624 | bytes 3968000 | tf_op jit(solution)/shard_map/oc,fchw->fohw/dot_general | solution.py:35
  95.5 2.6 %fusion.134 = f32[4,6,128,320]{2,3,1,0:T(8,128)} fusion(bf16[4,4,2,128]{3,1,2,0:T(4,128)(2,1)S(1)} %collective-permute-done.7, bf16[4,4,4,128]{3,1,2,0:T(4,128)(2,1)S(1)} %fusion.140, bf16[3,3,320,4]{2,3,1,0:T(4,128)(2,1)S(1)} %copy-done.6), kind=kOutput, calls=%fused_computation.174 | convolution fusion | flops 7913472 | bytes 3959808 | tf_op jit(solution)/shard_map/oc,fchw->fohw/dot_general | solution.py:35
  98.1 6.9 %fusion.9 = bf16[4,320,6,128]{3,1,2,0:T(8,128)(2,1)S(1)} fusion(f32[4,6,128,320]{2,3,1,0:T(8,128)} %fusion.134, f32[4,6,128,320]{2,3,1,0:T(8,128)} %fusion.120, f32[4,6,128,320]{2,3,1,0:T(8,128)S(1)} %fusion.119, f32[4,6,128,320]{2,3,1,0:T(8,128)} %fusion.155, f32[4,6,128,320]{2,3,1,0:T(8,128)S(1)} %fusion.118, f32[4,6,128,320]{2,3,1,0:T(8,128)S(1)} %fusion.117, ...), kind=kOutput, calls=%fused_computation.25 | convolution fusion | flops 21626880 | bytes 33459712 | tf_op jit(solution)/shard_map/oc,fchw->fohw/dot_general | solution.py:35
  105.0 2.0 %fusion.25 = f32[4,4,128,320]{2,3,1,0:T(8,128)S(1)} fusion(bf16[4,320,6,128]{3,1,2,0:T(8,128)(2,1)S(1)} %fusion.9, bf16[3,3,320,320]{3,2,1,0:T(8,128)(2,1)} %param.11), kind=kOutput, calls=%fused_computation.49 | convolution fusion | flops 419430400 | bytes 4833280 | tf_op jit(solution)/shard_map/oc,fchw->fohw/dot_general | solution.py:35
  107.1 0.9 fusion.26
  108.1 1.0 fusion.27
  109.0 0.9 fusion.28
  110.0 1.0 fusion.29
  110.9 0.8 fusion.34
  111.8 0.8 fusion.36
  112.6 0.8 fusion.38
  113.5 3.8 %fusion.19 = (bf16[4,320,4,128]{3,1,2,0:T(8,128)(2,1)S(1)}, f32[4,4,128,320]{2,3,1,0:T(8,128)}) fusion(bf16[4,320,6,128]{3,1,2,0:T(8,128)(2,1)S(1)} %fusion.9, bf16[3,3,320,320]{3,2,1,0:T(8,128)(2,1)S(1)} %copy-done.2, f32[4,4,128,320]{2,3,1,0:T(8,128)S(1)} %fusion.34, f32[4,4,128,320]{2,3,1,0:T(8,128)S(1)} %fusion.29, f32[4,4,128,320]{2,3,1,0:T(8,128)S(1)} %fusion.28, ...), kind=kOutput, calls=%fused_computation.43 | convolution fusion | flops 427950080 | bytes 27115520 | tf_op jit(solution)/shard_map/oc,fchw->fohw/dot_general | solution.py:35
  117.4 5.0 %collective-permute-start.8 = (bf16[1,320,4,128]{3,1,2,0:T(8,128)(2,1)S(1)}, bf16[1,320,4,128]{3,1,2,0:T(8,128)(2,1)S(1)}, u32[]{:S(2)}, u32[]{:S(2)}) collective-permute-start(bf16[1,320,4,128]{3,1,2,0:T(8,128)(2,1)S(1)} %get-tuple-element.6), channel_id=1, source_target_pairs={{0,64},{64,128},{128,192},{1,65},{65,129},{129,193},{2,66},{66,130... | collective-permute-start | bytes 983048 | tf_op jit(solution)/shard_map/ppermute | solution.py:14
  122.4 1.9 %collective-permute-start.9 = (bf16[1,320,4,128]{3,1,2,0:T(8,128)(2,1)S(1)}, bf16[1,320,4,128]{3,1,2,0:T(8,128)(2,1)S(1)}, u32[]{:S(2)}, u32[]{:S(2)}) collective-permute-start(bf16[1,320,4,128]{3,1,2,0:T(8,128)(2,1)S(1)} %get-tuple-element.5), channel_id=1, source_target_pairs={{64,0},{128,64},{192,128},{65,1},{129,65},{193,129},{66,2},{130,66... | collective-permute-start | bytes 983048 | tf_op jit(solution)/shard_map/ppermute | solution.py:17
  124.3 2.3 %fusion.62 = f32[4,4,128,320]{2,3,1,0:T(8,128)} fusion(bf16[4,320,4,128]{3,1,2,0:T(8,128)(2,1)S(1)} %get-tuple-element.21, bf16[3,320,320]{2,1,0:T(8,128)(2,1)S(1)} %copy-done.4), kind=kOutput, calls=%fused_computation.88 | convolution fusion | flops 419430400 | bytes 4177920 | tf_op jit(solution)/shard_map/oc,fchw->fohw/dot_general | solution.py:50
  126.7 2.4 %fusion.32 = f32[4,4,128,320]{2,3,1,0:T(8,128)} fusion(bf16[4,320,4,128]{3,1,2,0:T(8,128)(2,1)S(1)} %get-tuple-element.21, bf16[1,320,4,128]{3,1,2,0:T(8,128)(2,1)S(1)} %collective-permute-done.8, bf16[3,320,320]{2,1,0:T(8,128)(2,1)S(1)} %copy-done.4), kind=kOutput, calls=%fused_computation.58 | convolution fusion | flops 422051840 | bytes 4505600 | tf_op jit(solution)/shard_map/oc,fchw->fohw/dot_general | solution.py:47
  129.1 1.7 %collective-permute-done.9 = bf16[1,320,4,128]{3,1,2,0:T(8,128)(2,1)S(1)} collective-permute-done((bf16[1,320,4,128]{3,1,2,0:T(8,128)(2,1)S(1)}, bf16[1,320,4,128]{3,1,2,0:T(8,128)(2,1)S(1)}, u32[]{:S(2)}, u32[]{:S(2)}) %collective-permute-start.9) | collective-permute-done | bytes 327712 | tf_op jit(solution)/shard_map/ppermute | solution.py:17
  130.8 4.5 %fusion.138 = bf16[1,4,4,4,128]{4,2,3,1,0:T(4,128)(2,1)S(1)} fusion(bf16[4,4,4,128]{3,1,2,0:T(4,128)(2,1)S(1)} %fusion.140, f32[4,4,128,320]{2,3,1,0:T(8,128)} %get-tuple-element.22, f32[4,4,128,320]{2,3,1,0:T(8,128)} %fusion.32, f32[4,4,128,320]{2,3,1,0:T(8,128)} %fusion.62, bf16[1,320,4,128]{3,1,2,0:T(8,128)(2,1)S(1)} %collective-permute-done.9, ...), kind=kOutput, calls=%fused_computation.178 | convolution fusion | flops 429957120 | bytes 9783840 | tf_op jit(solution)/shard_map/oc,fchw->fohw/dot_general | solution.py:84
  135.3 0.6 copy.12
  (38 shorter events, 0.3 us)
Async XLA Ops:
  0.0 65.2 %copy-start = (bf16[4,320]{1,0:T(4,128)(2,1)S(1)}, bf16[4,320]{1,0:T(4,128)(2,1)}, u32[]{:S(2)}) copy-start(bf16[4,320]{1,0:T(4,128)(2,1)} %param.13) | copy-start | bytes 7684
  0.0 22.1 %copy-start.5 = (bf16[3,3,320,4]{2,3,1,0:T(4,128)(2,1)S(1)}, bf16[3,3,320,4]{2,3,1,0:T(4,128)(2,1)}, u32[]{:S(2)}) copy-start(bf16[3,3,320,4]{2,3,1,0:T(4,128)(2,1)} %param.10) | copy-start | bytes 69124
  0.8 7.4 %collective-permute-start = (bf16[4,4,4,128]{3,1,2,0:T(4,128)(2,1)S(1)}, bf16[4,4,4,128]{3,1,2,0:T(4,128)(2,1)S(1)}, u32[]{:S(2)}, u32[]{:S(2)}) collective-permute-start(bf16[4,4,4,128]{3,1,2,0:T(4,128)(2,1)S(1)} %bitcast.335), channel_id=1, source_target_pairs={{0,64},{64,128},{128,192},{1,65},{65,129},{129,193},{2,66},{66,130... | collective-permute-start | bytes 49160 | tf_op jit(solution)/shard_map/ppermute | solution.py:25
  8.2 11.7 %collective-permute-start.1 = (bf16[4,4,2,128]{3,1,2,0:T(4,128)(2,1)S(1)}, bf16[4,4,2,128]{3,1,2,0:T(4,128)(2,1)S(1)}, u32[]{:S(2)}, u32[]{:S(2)}) collective-permute-start(bf16[4,4,2,128]{3,1,2,0:T(4,128)(2,1)S(1)} %get-tuple-element.13), channel_id=1, source_target_pairs={{0,1},{1,2},{2,3},{3,4},{4,5},{5,6},{6,7},{7,8},{8,9},{9,10},{10,1... | collective-permute-start | bytes 24584 | tf_op jit(solution)/shard_map/ppermute | solution.py:14
  11.4 9.2 %collective-permute-start.2 = (bf16[4,4,2,128]{3,1,2,0:T(4,128)(2,1)S(1)}, bf16[4,4,2,128]{3,1,2,0:T(4,128)(2,1)S(1)}, u32[]{:S(2)}, u32[]{:S(2)}) collective-permute-start(bf16[4,4,2,128]{3,1,2,0:T(4,128)(2,1)S(1)} %get-tuple-element.14), channel_id=1, source_target_pairs={{1,0},{2,1},{3,2},{4,3},{5,4},{6,5},{7,6},{8,7},{9,8},{10,9},{11,1... | collective-permute-start | bytes 24584 | tf_op jit(solution)/shard_map/ppermute | solution.py:17
  41.6 2.1 %copy-start.1 = (bf16[3,3,320,320]{3,2,1,0:T(8,128)(2,1)S(1)}, bf16[3,3,320,320]{3,2,1,0:T(8,128)(2,1)}, u32[]{:S(2)}) copy-start(bf16[3,3,320,320]{3,2,1,0:T(8,128)(2,1)} %param.11) | copy-start | bytes 5529604
  50.1 8.6 %copy-start.3 = (bf16[3,320,320]{2,1,0:T(8,128)(2,1)S(1)}, bf16[3,320,320]{2,1,0:T(8,128)(2,1)}, u32[]{:S(2)}) copy-start(bf16[3,320,320]{2,1,0:T(8,128)(2,1)} %param.12) | copy-start | bytes 1843204
  54.0 7.1 %collective-permute-start.3 = (bf16[1,320,4,128]{3,1,2,0:T(8,128)(2,1)S(1)}, bf16[1,320,4,128]{3,1,2,0:T(8,128)(2,1)S(1)}, u32[]{:S(2)}, u32[]{:S(2)}) collective-permute-start(bf16[1,320,4,128]{3,1,2,0:T(8,128)(2,1)S(1)} %get-tuple-element.8), channel_id=1, source_target_pairs={{0,64},{64,128},{128,192},{1,65},{65,129},{129,193},{2,66},{66,130... | collective-permute-start | bytes 983048 | tf_op jit(solution)/shard_map/ppermute | solution.py:14
  56.8 8.4 %collective-permute-start.4 = (bf16[1,320,4,128]{3,1,2,0:T(8,128)(2,1)S(1)}, bf16[1,320,4,128]{3,1,2,0:T(8,128)(2,1)S(1)}, u32[]{:S(2)}, u32[]{:S(2)}) collective-permute-start(bf16[1,320,4,128]{3,1,2,0:T(8,128)(2,1)S(1)} %get-tuple-element.7), channel_id=1, source_target_pairs={{64,0},{128,64},{192,128},{65,1},{129,65},{193,129},{66,2},{130,66... | collective-permute-start | bytes 983048 | tf_op jit(solution)/shard_map/ppermute | solution.py:17
  61.0 4.1 %copy-start.8 = (f32[4]{0:T(128)S(1)}, f32[4]{0:T(128)}, u32[]{:S(2)}) copy-start(f32[4]{0:T(128)} %get-tuple-element.25) | copy-start | bytes 52
  61.0 4.1 %copy-start.9 = (f32[4]{0:T(128)S(1)}, f32[4]{0:T(128)}, u32[]{:S(2)}) copy-start(f32[4]{0:T(128)} %get-tuple-element.26) | copy-start | bytes 52
  65.2 7.8 %copy-start.7 = (bf16[1,4,4,4,128]{4,3,2,1,0:T(4,128)(2,1)S(1)}, bf16[1,4,4,4,128]{4,3,2,1,0:T(4,128)(2,1)}, u32[]{:S(2)}) copy-start(bf16[1,4,4,4,128]{4,3,2,1,0:T(4,128)(2,1)} %get-tuple-element.9) | copy-start | bytes 49156
  65.2 19.6 %copy-start.6 = (bf16[3,3,320,4]{2,3,1,0:T(4,128)(2,1)S(1)}, bf16[3,3,320,4]{2,3,1,0:T(4,128)(2,1)}, u32[]{:S(2)}) copy-start(bf16[3,3,320,4]{2,3,1,0:T(4,128)(2,1)} %param.10) | copy-start | bytes 69124
  69.7 3.3 %collective-permute-start.5 = (bf16[4,4,4,128]{3,1,2,0:T(4,128)(2,1)S(1)}, bf16[4,4,4,128]{3,1,2,0:T(4,128)(2,1)S(1)}, u32[]{:S(2)}, u32[]{:S(2)}) collective-permute-start(bf16[4,4,4,128]{3,1,2,0:T(4,128)(2,1)S(1)} %subtract_convert_fusion.1), channel_id=1, source_target_pairs={{0,64},{64,128},{128,192},{1,65},{65,129},{129,193},{2,66},{66,130... | collective-permute-start | bytes 49160 | tf_op jit(solution)/shard_map/ppermute | solution.py:25
  73.0 11.7 %collective-permute-start.6 = (bf16[4,4,2,128]{3,1,2,0:T(4,128)(2,1)S(1)}, bf16[4,4,2,128]{3,1,2,0:T(4,128)(2,1)S(1)}, u32[]{:S(2)}, u32[]{:S(2)}) collective-permute-start(bf16[4,4,2,128]{3,1,2,0:T(4,128)(2,1)S(1)} %get-tuple-element.11), channel_id=1, source_target_pairs={{0,1},{1,2},{2,3},{3,4},{4,5},{5,6},{6,7},{7,8},{8,9},{9,10},{10,1... | collective-permute-start | bytes 24584 | tf_op jit(solution)/shard_map/ppermute | solution.py:14
  74.9 9.8 %collective-permute-start.7 = (bf16[4,4,2,128]{3,1,2,0:T(4,128)(2,1)S(1)}, bf16[4,4,2,128]{3,1,2,0:T(4,128)(2,1)S(1)}, u32[]{:S(2)}, u32[]{:S(2)}) collective-permute-start(bf16[4,4,2,128]{3,1,2,0:T(4,128)(2,1)S(1)} %get-tuple-element.12), channel_id=1, source_target_pairs={{1,0},{2,1},{3,2},{4,3},{5,4},{6,5},{7,6},{8,7},{9,8},{10,9},{11,1... | collective-permute-start | bytes 24584 | tf_op jit(solution)/shard_map/ppermute | solution.py:17
  105.0 2.1 %copy-start.2 = (bf16[3,3,320,320]{3,2,1,0:T(8,128)(2,1)S(1)}, bf16[3,3,320,320]{3,2,1,0:T(8,128)(2,1)}, u32[]{:S(2)}) copy-start(bf16[3,3,320,320]{3,2,1,0:T(8,128)(2,1)} %param.11) | copy-start | bytes 5529604
  113.5 10.9 %copy-start.4 = (bf16[3,320,320]{2,1,0:T(8,128)(2,1)S(1)}, bf16[3,320,320]{2,1,0:T(8,128)(2,1)}, u32[]{:S(2)}) copy-start(bf16[3,320,320]{2,1,0:T(8,128)(2,1)} %param.12) | copy-start | bytes 1843204
  117.4 9.3 %collective-permute-start.8 = (bf16[1,320,4,128]{3,1,2,0:T(8,128)(2,1)S(1)}, bf16[1,320,4,128]{3,1,2,0:T(8,128)(2,1)S(1)}, u32[]{:S(2)}, u32[]{:S(2)}) collective-permute-start(bf16[1,320,4,128]{3,1,2,0:T(8,128)(2,1)S(1)} %get-tuple-element.6), channel_id=1, source_target_pairs={{0,64},{64,128},{128,192},{1,65},{65,129},{129,193},{2,66},{66,130... | collective-permute-start | bytes 983048 | tf_op jit(solution)/shard_map/ppermute | solution.py:14
  122.4 8.4 %collective-permute-start.9 = (bf16[1,320,4,128]{3,1,2,0:T(8,128)(2,1)S(1)}, bf16[1,320,4,128]{3,1,2,0:T(8,128)(2,1)S(1)}, u32[]{:S(2)}, u32[]{:S(2)}) collective-permute-start(bf16[1,320,4,128]{3,1,2,0:T(8,128)(2,1)S(1)} %get-tuple-element.5), channel_id=1, source_target_pairs={{64,0},{128,64},{192,128},{65,1},{129,65},{193,129},{66,2},{130,66... | collective-permute-start | bytes 983048 | tf_op jit(solution)/shard_map/ppermute | solution.py:17
  126.7 4.1 %copy-start.10 = (f32[4]{0:T(128)S(1)}, f32[4]{0:T(128)}, u32[]{:S(2)}) copy-start(f32[4]{0:T(128)} %get-tuple-element.23) | copy-start | bytes 52
  126.7 4.1 %copy-start.11 = (f32[4]{0:T(128)S(1)}, f32[4]{0:T(128)}, u32[]{:S(2)}) copy-start(f32[4]{0:T(128)} %get-tuple-element.24) | copy-start | bytes 52
where the time goes:
time: 137 us; the launch traced here: 136 us
  matrix products  84 us (61%)
  starting transfers between devices  41 us (30%)
  local copies, waits for them, and re-layouts  5.35 us (4%)
  waiting for transfers between devices  5.05 us (4%)
    dot_general x36, matrix products, conv_rows(): jnp.einsum('oc,fchw->fohw', weight[row_tap, col_tap], window, preferred_e...  65.5 us
    ppermute x4, starting transfers between devices, with_halo(): lax.ppermute(lax.slice_in_dim(block, 0, width, axis=dim), axis, backward)  21.6 us
    ppermute x4, starting transfers between devices, with_halo(): lax.ppermute(lax.slice_in_dim(block, block.shape[dim] - width, None, axis...  12.9 us
    dot_general x2, matrix products, per_device(): jnp.einsum('oc,fchw->fohw', out_proj, predicted, preferred_element_type=j...  8.98 us
    ppermute x2, starting transfers between devices, shifted(): lax.ppermute(value, axis, [(source, source + steps) for source in range(l...  6.5 us
    dot_general x2, matrix products, time_terms(): jnp.einsum('oc,fchw->fohw', time_weight[0], extended[0:frame_count], pref...  4.79 us
    dot_general x2, matrix products, time_terms(): jnp.einsum('oc,fchw->fohw', time_weight[1], extended[1:frame_count + 1],...  4.69 us
    ppermute x4, waiting for transfers between devices, with_halo(): lax.ppermute(lax.slice_in_dim(block, 0, width, axis=dim), axis, backward)  4.19 us
  transfers between devices with their start and end apart: 10, of which 4 were waited for; matrix products, arithmetic and copies ran while one was open for 10% of the time, Pallas kernels for 0%

commit v1 on v0

v1 whole, which is shorter than its diff:
```python
import functools

import jax
import jax.numpy as jnp
from jax import lax
from jax.experimental import pallas as pl
from jax.experimental.pallas import tpu as pltpu
from jax.sharding import PartitionSpec as P

STEPS = 2
CH = 320
COLS = 128
ORDER = (0, 3, 1, 2)
F32 = jnp.float32
BF16 = jnp.bfloat16
MESH = pl.DeviceIdType.MESH


def block_of(frame):
    return ORDER.index(frame)


def shifted_cols(value, amount):
    lane = lax.broadcasted_iota(jnp.int32, value.shape, 1)
    rolled = pltpu.roll(value, amount % COLS, 1)
    edge = 0 if amount == 1 else COLS - 1
    return jnp.where(lane == edge, jnp.zeros_like(rolled), rolled)


def spread(source, index, target, base):
    for frame in range(4):
        for channel in range(4):
            piece = source[index + (frame, channel)].astype(F32)
            target[block_of(frame), pl.ds(base + channel, 4, stride=4), :] = piece


def prepare_first(cf, w1t, w1, top_mask, bottom_mask):
    w1t[...] = jnp.zeros_like(w1t)
    for row_tap in range(3):
        for col_tap in range(3):
            place = col_tap * 32 + row_tap * 4
            w1t[place : place + 4, 0:CH] = cf[row_tap * 3 + col_tap].astype(F32) * 0.5
    base = jnp.transpose(w1t[...])[0:CH]
    for row in range(6):
        value = pltpu.roll(base, 4 * row, 1) if row else base
        if row == 0:
            value = value * top_mask
        if row == 5:
            value = value * bottom_mask
        w1[row * CH : (row + 1) * CH, :] = value.astype(BF16)


def prepare_second(cs, wcat):
    for tap in range(9):
        wcat[:, tap * CH : (tap + 1) * CH] = cs[tap] * jnp.asarray(0.5, BF16)


def prepare_projection(op, tw, p16, pst):
    p16[...] = jnp.zeros_like(p16)
    p16[0:4, :] = op[...].astype(F32)
    p16[12:16, :] = op[...].astype(F32)
    both = p16[...].astype(BF16)
    pst[...] = jnp.zeros_like(pst)
    through = [jnp.dot(both, tw[k], preferred_element_type=F32) for k in range(3)]
    for odd in range(2):
        rows = slice(odd * 8, odd * 8 + 8)
        pst[odd, 0:8, 0:CH] = p16[rows, :] * 2.0
        for place, k in enumerate((1, 0, 2)):
            pst[odd, place * 8 : place * 8 + 8, 384 : 384 + CH] = through[k][rows]


def window_columns(q, x1):
    for block in range(4):
        lanes = slice(block * COLS, (block + 1) * COLS)
        value = q[block]
        x1[0:32, lanes] = shifted_cols(value, 1).astype(BF16)
        x1[32:64, lanes] = value.astype(BF16)
        x1[64:96, lanes] = shifted_cols(value, -1).astype(BF16)


def first_row(row, pair, x1, w1, stack):
    half = jnp.dot(
        w1[row * CH : (row + 1) * CH, 0:96], x1[:, pair * 256 : pair * 256 + 256], preferred_element_type=F32
    )
    act = half + half * jnp.tanh(half)
    for block in range(2):
        lanes = slice(block * COLS, (block + 1) * COLS)
        piece = act[:, lanes]
        base = row * 3 * CH
        stack[pair, base : base + CH, lanes] = shifted_cols(piece, 1).astype(BF16)
        stack[pair, base + CH : base + 2 * CH, lanes] = piece.astype(BF16)
        stack[pair, base + 2 * CH : base + 3 * CH, lanes] = shifted_cols(piece, -1).astype(BF16)


def second_row(row, pair, wcat, stack, pst, held, sums):
    half = jnp.dot(
        wcat[...], stack[pair, row * 3 * CH : (row + 3) * 3 * CH, :], preferred_element_type=F32
    )
    slot = pair * 4 + row
    held[slot, 0:CH, :] = half.astype(BF16)
    held[slot, 384 : 384 + CH, :] = (half + half * jnp.tanh(half)).astype(BF16)
    terms = jnp.dot(pst[row % 2].astype(BF16), held[slot], preferred_element_type=F32)
    rows = slice(8 * (row // 2), 8 * (row // 2) + 8)
    for place in range(3):
        term = terms[place * 8 : place * 8 + 8]
        if row % 2:
            sums[pair, place, rows, :] += term
        else:
            sums[pair, place, rows, :] = term


def part(sums, place, frame):
    block = block_of(frame)
    return sums[block // 2, place, :, (block % 2) * COLS : (block % 2 + 1) * COLS]


def kernel(levels, tiles, comm, queue_hbm, noise_hbm, cf_hbm, cs_hbm, tw_hbm, op_hbm, keep, rate, out,
           qin, nin, cf, cs, tw, op, wcat, w1t, w1, p16, pst, q, stage, x1, stack, held, sums,
           lo_send, hi_send, lo_recv, hi_recv, load_sem, send_sem, recv_sem):
    if comm:
        g, t = lax.axis_index("level"), lax.axis_index("tile")
    else:
        g, t = jnp.int32(0), jnp.int32(1)

    loads = [
        pltpu.make_async_copy(source, target, load_sem.at[i])
        for i, (source, target) in enumerate(
            [(queue_hbm, qin), (noise_hbm, nin), (cf_hbm, cf), (op_hbm, op), (tw_hbm, tw), (cs_hbm, cs)]
        )
    ]
    for load in loads:
        load.start()

    has_up, has_down = t > 0, t < tiles - 1
    not_last = g < levels - 1

    if comm:
        barrier = pltpu.get_barrier_semaphore()
        count = jnp.int32(0)
        for dg in (-1, 0, 1):
            for dt in (-1, 0, 1):
                if dg == 0 and dt == 0:
                    continue
                ok = (g + dg >= 0) & (g + dg < levels) & (t + dt >= 0) & (t + dt < tiles)
                if dg == 0:
                    ok = ok & (g == 0)

                @pl.when(ok)
                def _(dg=dg, dt=dt):
                    pl.semaphore_signal(barrier, inc=1, device_id=(g + dg, t + dt), device_id_type=MESH)

                count = count + ok.astype(jnp.int32)

    loads[0].wait()
    loads[1].wait()
    spread(qin, (), stage.at[0], 0)

    @pl.when(g == 0)
    def _():
        for step in range(STEPS):
            spread(nin, (step,), q.at[step], 8)

    for step in range(STEPS):
        @pl.when(jnp.logical_not(has_up))
        def _(step=step):
            q[step, :, 0:8, :] = jnp.zeros((4, 8, COLS), F32)

        @pl.when(jnp.logical_not(has_down))
        def _(step=step):
            q[step, :, 24:32, :] = jnp.zeros((4, 8, COLS), F32)

    def shift_copies(step):
        pairs = [
            (stage.at[step], q.at[step, :, 8:24, :], 0, not_last),
            (stage.at[step, :, 8:16, :], q.at[step, :, 0:8, :], 1, not_last & has_down),
            (stage.at[step, :, 0:8, :], q.at[step, :, 24:32, :], -1, not_last & has_up),
        ]
        return [
            (ok, pltpu.make_async_remote_copy(
                src_ref=src, dst_ref=dst, send_sem=send_sem.at[step, i], recv_sem=recv_sem.at[step, i],
                device_id=(g + 1, t + dt), device_id_type=MESH))
            for i, (src, dst, dt, ok) in enumerate(pairs)
        ]

    def noise_copies(step):
        pairs = [
            (q.at[step, :, 16:24, :], q.at[step, :, 0:8, :], 1, (g == 0) & has_down),
            (q.at[step, :, 8:16, :], q.at[step, :, 24:32, :], -1, (g == 0) & has_up),
        ]
        return [
            (ok, pltpu.make_async_remote_copy(
                src_ref=src, dst_ref=dst, send_sem=send_sem.at[step, 3 + i], recv_sem=recv_sem.at[step, 1 + i],
                device_id=(g, t + dt), device_id_type=MESH))
            for i, (src, dst, dt, ok) in enumerate(pairs)
        ]

    def term_copies(step):
        pairs = [
            (lo_send.at[step], hi_recv.at[step], -1, g > 0),
            (hi_send.at[step], lo_recv.at[step], 1, not_last),
        ]
        return [
            (ok, pltpu.make_async_remote_copy(
                src_ref=src, dst_ref=dst, send_sem=send_sem.at[step, 5 + i], recv_sem=recv_sem.at[step, 3 + i],
                device_id=(g + dg, t), device_id_type=MESH))
            for i, (src, dst, dg, ok) in enumerate(pairs)
        ]

    def start(copies):
        for ok, copy in copies:
            @pl.when(ok)
            def _(copy=copy):
                copy.start()

    def wait_send(copies):
        for ok, copy in copies:
            @pl.when(ok)
            def _(copy=copy):
                copy.wait_send()

    def wait_latents(step):
        copies = [copy for _, copy in shift_copies(step)]
        for copy, ok in zip(copies, (g > 0, has_up, has_down)):
            @pl.when(ok)
            def _(copy=copy):
                copy.wait_recv()

    def wait_terms(step):
        copies = [copy for _, copy in term_copies(step)]
        for copy, ok in zip(copies, (not_last, g > 0)):
            @pl.when(ok)
            def _(copy=copy):
                copy.wait_recv()

    if comm:
        pl.semaphore_wait(barrier, count)
        start(shift_copies(0))
        start(noise_copies(0))
        start(noise_copies(1))

    for step in range(STEPS):
        @pl.when(g == 0)
        def _(step=step):
            lo_recv[step] = jnp.zeros((16, COLS), F32)

        @pl.when(jnp.logical_not(not_last))
        def _(step=step):
            hi_recv[step] = jnp.zeros((16, COLS), F32)

    for slot in range(8):
        held[slot, CH:384, :] = jnp.zeros((64, 256), BF16)
    loads[2].wait()
    prepare_first(cf, w1t, w1, has_up.astype(F32), has_down.astype(F32))
    loads[3].wait()
    loads[4].wait()
    prepare_projection(op, tw, p16, pst)
    loads[5].wait()
    prepare_second(cs, wcat)

    for step in range(STEPS):
        now = q.at[step]
        if comm:
            wait_latents(step)
        window_columns(now, x1)
        for pair in range(2):
            for row in range(6):
                first_row(row, pair, x1, w1, stack)
            for row in range(4):
                second_row(row, pair, wcat, stack, pst, held, sums)
            if pair == 0:
                lo_send[step] = part(sums, 2, 0)
                hi_send[step] = part(sums, 1, 3)
                if comm:
                    start(term_copies(step))
        if comm:
            wait_terms(step)
        for frame in range(4):
            block = block_of(frame)
            before = lo_recv[step] if frame == 0 else part(sums, 1, frame - 1)
            after = hi_recv[step] if frame == 3 else part(sums, 2, frame + 1)
            projected = part(sums, 0, frame) + before + after
            fresh = keep[step, g, frame] * now[block, 8:24, :] - rate[step, g, frame] * projected
            stage[step + 1, block] = fresh.astype(BF16).astype(F32)
        if step + 1 < STEPS and comm:
            start(shift_copies(step + 1))

    for frame in range(4):
        for channel in range(4):
            out[frame, channel] = stage[STEPS, block_of(frame), pl.ds(channel, 4, stride=4), :].astype(BF16)

    if comm:
        for step in range(STEPS):
            wait_send(shift_copies(step))
            wait_send(noise_copies(step))
            wait_send(term_copies(step))


def call(levels, tiles, comm, *args):
    hbm = pl.BlockSpec(memory_space=pltpu.HBM)
    smem = pl.BlockSpec(memory_space=pltpu.SMEM)
    scratch = [
        pltpu.VMEM((4, 4, 4, COLS), BF16),
        pltpu.VMEM((2, 4, 4, 4, COLS), BF16),
        pltpu.VMEM((9, 4, CH), BF16),
        pltpu.VMEM((9, CH, CH), BF16),
        pltpu.VMEM((3, CH, CH), BF16),
        pltpu.VMEM((4, CH), BF16),
        pltpu.VMEM((CH, 9 * CH), BF16),
        pltpu.VMEM((COLS, 384), F32),
        pltpu.VMEM((6 * CH, COLS), BF16),
        pltpu.VMEM((16, CH), F32),
        pltpu.VMEM((2, 32, 704), F32),
        pltpu.VMEM((STEPS, 4, 32, COLS), F32),
        pltpu.VMEM((STEPS + 1, 4, 16, COLS), F32),
        pltpu.VMEM((96, 512), BF16),
        pltpu.VMEM((2, 18 * CH, 256), BF16),
        pltpu.VMEM((8, 704, 256), BF16),
        pltpu.VMEM((2, 3, 16, 256), F32),
        pltpu.VMEM((STEPS, 16, COLS), F32),
        pltpu.VMEM((STEPS, 16, COLS), F32),
        pltpu.VMEM((STEPS, 16, COLS), F32),
        pltpu.VMEM((STEPS, 16, COLS), F32),
        pltpu.SemaphoreType.DMA((6,)),
        pltpu.SemaphoreType.DMA((STEPS, 7)),
        pltpu.SemaphoreType.DMA((STEPS, 5)),
    ]
    return pl.pallas_call(
        functools.partial(kernel, levels, tiles, comm),
        out_shape=jax.ShapeDtypeStruct((4, 4, 4, COLS), BF16),
        in_specs=[hbm] * 6 + [smem] * 2,
        out_specs=pl.BlockSpec(memory_space=pltpu.VMEM),
        scratch_shapes=scratch,
        compiler_params=pltpu.CompilerParams(
            vmem_limit_bytes=62 << 20,
            **(dict(collective_id=0, has_side_effects=True) if comm else {}),
        ),
        name="queue_steps",
    )(*args)


def per_device(levels, tiles, queue_init, noise_frames, conv_first, conv_second, time_weight, out_proj, keep_coef, noise_coef):
    out = call(
        levels, tiles, True, queue_init[0], noise_frames, jnp.transpose(conv_first, (0, 1, 3, 2)).reshape(9, 4, CH), conv_second.reshape(9, CH, CH),
        time_weight, out_proj, keep_coef, noise_coef,
    )
    return out[None]


def solution(mesh):
    return jax.shard_map(
        functools.partial(per_device, mesh.shape["level"], mesh.shape["tile"]),
        mesh=mesh,
        in_specs=(
            P("level", None, None, "tile", None),
            P(None, None, None, "tile", None),
            P(),
            P(),
            P(),
            P(),
            P(),
            P(),
        ),
        out_specs=P("level", None, None, "tile", None),
        check_vma=False,
    )
```

time: 137 us -> 40.6 us (0.30)
  matrix products: 84 us -> 0 us
  starting transfers between devices: 41 us -> 0 us
  Pallas kernels: 0 us -> 38.9 us
  waiting for transfers between devices: 5.05 us -> 0 us
  local copies, waits for them, and re-layouts: 5.35 us -> 1.33 us
    dot_general x42 -> x0, matrix products: 84 us -> none  [the longest x36 65.5 us: conv_rows(): jnp.einsum('oc,fchw->fohw', weight[row_tap, col_tap], window, preferred_e...]
    ppermute x10 -> x0, starting transfers between devices: 41 us -> none  [the longest x4 21.6 us: with_halo(): lax.ppermute(lax.slice_in_dim(block, 0, width, axis=dim), axis, backward)]
    pallas_call x0 -> x1, Pallas kernels: none -> 38.9 us  [call(): pl.pallas_call(functools.partial(kernel, levels, tiles, comm), out_shape=...]
    ppermute x10 -> x0, waiting for transfers between devices: 5.05 us -> none  [the longest x4 4.19 us: with_halo(): lax.ppermute(lax.slice_in_dim(block, 0, width, axis=dim), axis, backward)]
    slice x7 -> x0, local copies, waits for them, and re-layouts: 2.86 us -> none  [the longest x1 1.36 us: per_device(): queued = jnp.where(position == 0, noise_frames[step_index], queued)]
  transfers between devices with their start and end apart: 10 -> 0, of which waited for: 4 -> 0; matrix products, arithmetic and copies ran while one was open for 10% -> 0% of each run, Pallas kernels for 0% -> 0%
where the time goes in v1:
time: 40.6 us; the launch traced here: 40.2 us
  Pallas kernels  38.9 us (96%)
  local copies, waits for them, and re-layouts  1.33 us (3%)
    pallas_call x1, Pallas kernels, call(): pl.pallas_call(functools.partial(kernel, levels, tiles, comm), out_shape=...  38.9 us
    unnamed x1, local copies, waits for them, and re-layouts  1.33 us

profile of v1, /device:TPU:7, one launch (start us, length us, event | category | flops | bytes accessed | tf_op | source)
XLA Modules:
  0.0 40.2 jit_solution(14776241679102989424)
XLA Ops:
  0.0 38.9 %queue_steps.1 = bf16[4,4,4,128]{3,2,1,0:T(4,128)(2,1)} custom-call(bf16[4,4,4,128]{3,2,1,0:T(4,128)(2,1)} %bitcast.9, bf16[2,4,4,4,128]{4,3,2,1,0:T(4,128)(2,1)} %noise_hbm.1, bf16[9,4,320]{2,1,0:T(4,128)(2,1)} %bitcast.8, bf16[9,320,320]{2,1,0:T(8,128)(2,1)} %bitcast.6, bf16[3,320,320]{2,1,0:T(8,128)(2,1)} %tw_hbm.1, bf16[4,320]{1,0:T(4,128)(2,1)} %op_hbm.1, ...), custom_call_target="tpu_custom_call" | custom-call | tf_op jit(solution)/shard_map/queue_steps/pallas_call | solution.py:327
  38.9 1.3 %copy.10 = bf16[1,4,4,4,128]{4,3,2,1,0:T(4,128)(2,1)} copy(bf16[1,4,4,4,128]{4,3,2,1,0:T(4,128)(2,1)} %bitcast.7) | data formatting | bytes 32768

commit v2 on v1

v2 whole, which is shorter than its diff:
```python
import functools

import jax
import jax.numpy as jnp
from jax import lax
from jax.experimental import pallas as pl
from jax.experimental.pallas import tpu as pltpu
from jax.sharding import PartitionSpec as P

STEPS = 2
CH = 320
COLS = 128
ORDER = (0, 3, 1, 2)
F32 = jnp.float32
BF16 = jnp.bfloat16
MESH = pl.DeviceIdType.MESH


def block_of(frame):
    return ORDER.index(frame)


def shifted_cols(value, amount):
    lane = lax.broadcasted_iota(jnp.int32, value.shape, 1)
    rolled = pltpu.roll(value, amount % COLS, 1)
    edge = 0 if amount == 1 else COLS - 1
    return jnp.where(lane == edge, jnp.zeros_like(rolled), rolled)


def spread(source, index, target):
    for frame in range(4):
        for channel in range(4):
            piece = source[index + (frame, channel)].astype(F32)
            target[block_of(frame), pl.ds(channel, 4, stride=4), :] = piece


def prepare_first(cf, w1t, w1, top_mask, bottom_mask):
    w1t[...] = jnp.zeros_like(w1t)
    for row_tap in range(3):
        for col_tap in range(3):
            place = col_tap * 32 + row_tap * 4
            w1t[place : place + 4, 0:CH] = cf[row_tap * 3 + col_tap].astype(F32) * 0.5
    base = jnp.transpose(w1t[...])[0:CH]
    for row in range(6):
        value = pltpu.roll(base, 4 * row, 1) if row else base
        if row == 0:
            value = value * top_mask
        if row == 5:
            value = value * bottom_mask
        w1[row * CH : (row + 1) * CH, :] = value.astype(BF16)


def prepare_second(cs, wt):
    for col_tap in range(3):
        lanes = slice(col_tap * CH, (col_tap + 1) * CH)
        g0, g1, g2 = (cs[a * 3 + col_tap].astype(F32) for a in range(3))
        outer = 0.25 * (g0 + g2)
        wt[0, :, lanes] = (0.5 * g0).astype(BF16)
        wt[1, :, lanes] = (outer + 0.25 * g1).astype(BF16)
        wt[2, :, lanes] = (outer - 0.25 * g1).astype(BF16)
        wt[3, :, lanes] = (0.5 * g2).astype(BF16)


def prepare_projection(op, tw, p16, pst):
    p16[...] = jnp.zeros_like(p16)
    p16[0:4, :] = op[...].astype(F32)
    p16[12:16, :] = op[...].astype(F32)
    both = p16[...].astype(BF16)
    pst[...] = jnp.zeros_like(pst)
    through = [jnp.dot(both, tw[k], preferred_element_type=F32) for k in range(3)]
    for odd in range(2):
        rows = slice(odd * 8, odd * 8 + 8)
        pst[odd, 0:8, 0:CH] = p16[rows, :] * 2.0
        for place, k in enumerate((1, 0, 2)):
            pst[odd, place * 8 : place * 8 + 8, 384 : 384 + CH] = through[k][rows]


def window_columns(half, q, x1):
    for block in range(4):
        lanes = slice(block * COLS, (block + 1) * COLS)
        if half == 0:
            value = jnp.concatenate([q[block, 0:24, :], jnp.zeros((8, COLS), F32)], axis=0)
        else:
            value = jnp.concatenate([jnp.zeros((8, COLS), F32), q[block, 8:32, :]], axis=0)
        x1[half, 0:32, lanes] = shifted_cols(value, 1).astype(BF16)
        x1[half, 32:64, lanes] = value.astype(BF16)
        x1[half, 64:96, lanes] = shifted_cols(value, -1).astype(BF16)


def first_row(row, half, pair, x1, w1, act):
    part = jnp.dot(
        w1[row * CH : (row + 1) * CH, 0:96], x1[half, :, pair * 256 : pair * 256 + 256], preferred_element_type=F32
    )
    act[pair, row] = (part + part * jnp.tanh(part)).astype(BF16)


def transform(half, pair, j, act, ust):
    left, right = ((0, 2), (1, 2), (2, 1), (1, 3))[j]
    for block in range(2):
        lanes = slice(block * COLS, (block + 1) * COLS)
        one = act[pair, 2 * half + left, :, lanes]
        two = act[pair, 2 * half + right, :, lanes]
        piece = one + two if j == 1 else one - two
        ust[half, pair, j, 0:CH, lanes] = shifted_cols(piece, 1)
        ust[half, pair, j, CH : 2 * CH, lanes] = piece
        ust[half, pair, j, 2 * CH : 3 * CH, lanes] = shifted_cols(piece, -1)


def product(half, pair, j, wt, ust, products):
    products[half, pair, j] = jnp.dot(wt[j], ust[half, pair, j], preferred_element_type=F32)


def second_rows(half, pair, products, held):
    for odd in range(2):
        one, two = products[half, pair, 1], products[half, pair, 2]
        value = products[half, pair, 0] + one + two if odd == 0 else one - two - products[half, pair, 3]
        held[half, pair, odd, 0:CH, :] = value.astype(BF16)
        held[half, pair, odd, 384 : 384 + CH, :] = (value + value * jnp.tanh(value)).astype(BF16)


def term_rows(half, pair, pst, held, sums):
    terms = [
        jnp.dot(pst[odd].astype(BF16), held[half, pair, odd], preferred_element_type=F32) for odd in range(2)
    ]
    total = terms[0] + terms[1]
    for place in range(3):
        sums[half, pair, place] = total[place * 8 : place * 8 + 8]


def part_of(sums, half, place, frame):
    block = block_of(frame)
    return sums[half, block // 2, place, :, (block % 2) * COLS : (block % 2 + 1) * COLS]


def kernel(levels, tiles, comm, queue_hbm, noise_hbm, cf_hbm, cs_hbm, tw_hbm, op_hbm, keep, rate, out,
           qin, nin, cf, cs, tw, op, wt, w1t, w1, p16, pst, q, stage, noise, zeros, x1, act, ust, products, held, sums,
           lo_send, hi_send, lo_recv, hi_recv, load_sem, send_sem, recv_sem, term_send_sem, term_recv_sem):
    if comm:
        g, t = lax.axis_index("level"), lax.axis_index("tile")
    else:
        g, t = jnp.int32(0), jnp.int32(1)
    has_up, has_down = t > 0, t < tiles - 1
    first_level, not_last = g == 0, g < levels - 1

    loads = [
        pltpu.make_async_copy(source, target, load_sem.at[i])
        for i, (source, target) in enumerate(
            [(queue_hbm, qin), (noise_hbm, nin), (cf_hbm, cf), (op_hbm, op), (tw_hbm, tw), (cs_hbm, cs)]
        )
    ]
    for load in loads:
        load.start()

    if comm:
        barrier = pltpu.get_barrier_semaphore()
        count = jnp.int32(0)
        for dg in (-1, 0, 1):
            for dt in (-1, 0, 1):
                if dg == 0 and dt == 0:
                    continue
                ok = (t + dt >= 0) & (t + dt < tiles)
                if dg == 0:
                    ok = ok & first_level

                @pl.when(ok)
                def _(dg=dg, dt=dt):
                    pl.semaphore_signal(
                        barrier, inc=1, device_id=(lax.rem(g + dg + levels, levels), t + dt), device_id_type=MESH
                    )

                count = count + ok.astype(jnp.int32)

    loads[0].wait()
    loads[1].wait()
    spread(qin, (), stage.at[0])
    for step in range(STEPS):
        spread(nin, (step,), noise.at[step])
    zeros[...] = jnp.zeros_like(zeros)

    def place(step, kind):
        start = (8, 16, 0, 24)[kind]
        return q.at[step, :, start : start + 8, :]

    def remote(source, step, kind, level, tile, send):
        return pltpu.make_async_remote_copy(
            src_ref=source, dst_ref=place(step, kind), send_sem=send_sem.at[step, send],
            recv_sem=recv_sem.at[step, kind], device_id=(level, tile), device_id_type=MESH,
        )

    def main_copy(step, half):
        return remote(stage.at[step, :, 8 * half : 8 * half + 8, :], step, half, g + 1, t, half)

    def halo_copy(step, half):
        source = stage.at[step, :, 8 * half : 8 * half + 8, :]
        return remote(source, step, 3 - half, g + 1, t + (1 if half else -1), 2 + half)

    def noise_copy(step, half):
        source = noise.at[step, :, 8 * half : 8 * half + 8, :]
        return remote(source, step, 3 - half, g, t + (1 if half else -1), 4 + half)

    def local_copy(source, step, kind):
        return pltpu.make_async_copy(source, place(step, kind), recv_sem.at[step, kind])

    def term_copies(step, half):
        return [
            pltpu.make_async_remote_copy(
                src_ref=source.at[step, half], dst_ref=target.at[step, half], send_sem=term_send_sem.at[step, half, i],
                recv_sem=term_recv_sem.at[step, half, i], device_id=(lax.rem(g + dg, levels), t), device_id_type=MESH,
            )
            for i, (source, target, dg) in enumerate([(lo_send, hi_recv, levels - 1), (hi_send, lo_recv, 1)])
        ]

    def neighbour(half):
        return has_down if half else has_up

    def start_shift(step, half):
        @pl.when(not_last)
        def _():
            main_copy(step, half).start()

            @pl.when(neighbour(half))
            def _():
                halo_copy(step, half).start()

    def wait_latents(step, kind):
        local_copy(zeros, step, kind).wait()

    if comm:
        @pl.when(first_level)
        def _():
            for step in range(STEPS):
                for half in range(2):
                    local_copy(noise.at[step, :, 8 * half : 8 * half + 8, :], step, half).start()

        for half in range(2):
            @pl.when(jnp.logical_not(neighbour(half)))
            def _(half=half):
                for step in range(STEPS):
                    local_copy(zeros, step, 2 + half).start()

        pl.semaphore_wait(barrier, count)
        for half in (1, 0):
            start_shift(0, half)
        for half in (1, 0):
            @pl.when(first_level & neighbour(half))
            def _(half=half):
                for step in range(STEPS):
                    noise_copy(step, half).start()

    for half in range(2):
        for pair in range(2):
            for odd in range(2):
                held[half, pair, odd, CH:384, :] = jnp.zeros((64, 256), BF16)
    loads[2].wait()
    prepare_first(cf, w1t, w1, has_up.astype(F32), has_down.astype(F32))
    loads[3].wait()
    loads[4].wait()
    prepare_projection(op, tw, p16, pst)
    loads[5].wait()
    prepare_second(cs, wt)

    lo_mask, hi_mask = (g > 0).astype(F32), not_last.astype(F32)
    for step in range(STEPS):
        now = q.at[step]
        early = 1 - step % 2
        late = 1 - early

        def send_terms(half):
            lo_send[step, half] = part_of(sums, half, 2, 0)
            hi_send[step, half] = part_of(sums, half, 1, 3)
            if comm:
                for copy in term_copies(step, half):
                    copy.start()

        def finish(half):
            if comm:
                for copy in term_copies(step, half):
                    copy.wait_recv()
            rows = slice(8 * half, 8 * half + 8)
            for frame in range(4):
                block = block_of(frame)
                before = lo_recv[step, half] * lo_mask if frame == 0 else part_of(sums, half, 1, frame - 1)
                after = hi_recv[step, half] * hi_mask if frame == 3 else part_of(sums, half, 2, frame + 1)
                projected = part_of(sums, half, 0, frame) + before + after
                latent = now[block, 8 + 8 * half : 16 + 8 * half, :]
                fresh = keep[step, g, frame] * latent - rate[step, g, frame] * projected
                stage[step + 1, block, rows, :] = fresh.astype(BF16).astype(F32)
            if comm and step + 1 < STEPS:
                start_shift(step + 1, half)

        if comm:
            for kind in (0, 1, 2 + early):
                wait_latents(step, kind)
        def first(half, pair, rows):
            for row in rows:
                first_row(row, half, pair, x1, w1, act)

        def shape(half, pair, j):
            transform(half, pair, j, act, ust)

        window_columns(early, now, x1)
        low = 2 * early
        units = [(early, 0), (early, 1), (late, 0), (late, 1)]
        fresh_rows = (0, 1) if early else (4, 5)
        rows_of = [(low, low + 2, low + 1, low + 3)] * 2 + [fresh_rows] * 2
        first(early, 0, rows_of[0])
        shape(early, 0, 0)
        for u, (half, pair) in enumerate(units):
            for j in range(4):
                if j == 1 and u == 1:
                    if comm:
                        wait_latents(step, 2 + late)
                    window_columns(late, now, x1)
                if j in (1, 2) and u < 3:
                    rows = rows_of[u + 1]
                    first(*units[u + 1], rows[: len(rows) // 2] if j == 1 else rows[len(rows) // 2 :])
                product(half, pair, j, wt, ust, products)
                if j < 3:
                    shape(half, pair, j + 1)
                elif u < 3:
                    shape(*units[u + 1], 0)
                if j == 0 and u:
                    second_rows(*units[u - 1], products, held)
                if j == 2 and u:
                    term_rows(*units[u - 1], pst, held, sums)
                    if u in (1, 3):
                        send_terms(early if u == 1 else late)
        second_rows(*units[3], products, held)
        finish(early)
        term_rows(late, 1, pst, held, sums)
        finish(late)

    for frame in range(4):
        for channel in range(4):
            out[frame, channel] = stage[STEPS, block_of(frame), pl.ds(channel, 4, stride=4), :].astype(BF16)

    if comm:
        for step in range(STEPS):
            for half in range(2):
                for copy in term_copies(step, half):
                    copy.wait_send()

                @pl.when(not_last)
                def _(step=step, half=half):
                    main_copy(step, half).wait_send()

                    @pl.when(neighbour(half))
                    def _():
                        halo_copy(step, half).wait_send()

                @pl.when(first_level & neighbour(half))
                def _(step=step, half=half):
                    noise_copy(step, half).wait_send()


def call(levels, tiles, comm, *args):
    hbm = pl.BlockSpec(memory_space=pltpu.HBM)
    smem = pl.BlockSpec(memory_space=pltpu.SMEM)
    scratch = [
        pltpu.VMEM((4, 4, 4, COLS), BF16),
        pltpu.VMEM((2, 4, 4, 4, COLS), BF16),
        pltpu.VMEM((9, 4, CH), BF16),
        pltpu.VMEM((9, CH, CH), BF16),
        pltpu.VMEM((3, CH, CH), BF16),
        pltpu.VMEM((4, CH), BF16),
        pltpu.VMEM((4, CH, 3 * CH), BF16),
        pltpu.VMEM((COLS, 384), F32),
        pltpu.VMEM((6 * CH, COLS), BF16),
        pltpu.VMEM((16, CH), F32),
        pltpu.VMEM((2, 32, 704), F32),
        pltpu.VMEM((STEPS, 4, 32, COLS), F32),
        pltpu.VMEM((STEPS + 1, 4, 16, COLS), F32),
        pltpu.VMEM((STEPS, 4, 16, COLS), F32),
        pltpu.VMEM((4, 8, COLS), F32),
        pltpu.VMEM((2, 96, 512), BF16),
        pltpu.VMEM((2, 6, CH, 256), BF16),
        pltpu.VMEM((2, 2, 4, 3 * CH, 256), BF16),
        pltpu.VMEM((2, 2, 4, CH, 256), F32),
        pltpu.VMEM((2, 2, 2, 704, 256), BF16),
        pltpu.VMEM((2, 2, 3, 8, 256), F32),
        pltpu.VMEM((STEPS, 2, 8, COLS), F32),
        pltpu.VMEM((STEPS, 2, 8, COLS), F32),
        pltpu.VMEM((STEPS, 2, 8, COLS), F32),
        pltpu.VMEM((STEPS, 2, 8, COLS), F32),
        pltpu.SemaphoreType.DMA((6,)),
        pltpu.SemaphoreType.DMA((STEPS, 6)),
        pltpu.SemaphoreType.DMA((STEPS, 4)),
        pltpu.SemaphoreType.DMA((STEPS, 2, 2)),
        pltpu.SemaphoreType.DMA((STEPS, 2, 2)),
    ]
    return pl.pallas_call(
        functools.partial(kernel, levels, tiles, comm),
        out_shape=jax.ShapeDtypeStruct((4, 4, 4, COLS), BF16),
        in_specs=[hbm] * 6 + [smem] * 2,
        out_specs=pl.BlockSpec(memory_space=pltpu.VMEM),
        scratch_shapes=scratch,
        compiler_params=pltpu.CompilerParams(
            vmem_limit_bytes=62 << 20,
            **(dict(collective_id=0, has_side_effects=True) if comm else {}),
        ),
        name="queue_steps",
    )(*args)


def per_device(levels, tiles, queue_init, noise_frames, conv_first, conv_second, time_weight, out_proj, keep_coef, noise_coef):
    out = call(
        levels, tiles, True, queue_init[0], noise_frames, jnp.transpose(conv_first, (0, 1, 3, 2)).reshape(9, 4, CH), conv_second.reshape(9, CH, CH),
        time_weight, out_proj, keep_coef, noise_coef,
    )
    return out[None]


def solution(mesh):
    return jax.shard_map(
        functools.partial(per_device, mesh.shape["level"], mesh.shape["tile"]),
        mesh=mesh,
        in_specs=(
            P("level", None, None, "tile", None),
            P(None, None, None, "tile", None),
            P(),
            P(),
            P(),
            P(),
            P(),
            P(),
        ),
        out_specs=P("level", None, None, "tile", None),
        check_vma=False,
    )
```

time: 40.6 us -> 36 us (0.89)
  Pallas kernels: 38.9 us -> 34.4 us
    pallas_call x1, Pallas kernels: 38.9 us -> 34.4 us  [call(): pl.pallas_call(functools.partial(kernel, levels, tiles, comm), out_shape=...]
where the time goes in v2:
time: 36 us; the launch traced here: 35.7 us
  Pallas kernels  34.4 us (96%)
  local copies, waits for them, and re-layouts  1.33 us (4%)
    pallas_call x1, Pallas kernels, call(): pl.pallas_call(functools.partial(kernel, levels, tiles, comm), out_shape=...  34.4 us
    unnamed x1, local copies, waits for them, and re-layouts  1.33 us

profile of v2, /device:TPU:7, one launch (start us, length us, event | category | flops | bytes accessed | tf_op | source)
XLA Modules:
  0.0 35.7 jit_solution(9001634732905186657)
XLA Ops:
  0.0 34.4 %queue_steps.1 = bf16[4,4,4,128]{3,2,1,0:T(4,128)(2,1)} custom-call(bf16[4,4,4,128]{3,2,1,0:T(4,128)(2,1)} %bitcast.9, bf16[2,4,4,4,128]{4,3,2,1,0:T(4,128)(2,1)} %noise_hbm.1, bf16[9,4,320]{2,1,0:T(4,128)(2,1)} %bitcast.8, bf16[9,320,320]{2,1,0:T(8,128)(2,1)} %bitcast.6, bf16[3,320,320]{2,1,0:T(8,128)(2,1)} %tw_hbm.1, bf16[4,320]{1,0:T(4,128)(2,1)} %op_hbm.1, ...), custom_call_target="tpu_custom_call" | custom-call | tf_op jit(solution)/shard_map/queue_steps/pallas_call | solution.py:391
  34.4 1.3 %copy.10 = bf16[1,4,4,4,128]{4,3,2,1,0:T(4,128)(2,1)} copy(bf16[1,4,4,4,128]{4,3,2,1,0:T(4,128)(2,1)} %bitcast.7) | data formatting | bytes 32768

commit v3 on v2

--- a/solution.py
+++ b/solution.py
@@ -171,10 +171,7 @@
                 count = count + ok.astype(jnp.int32)
 
     loads[0].wait()
-    loads[1].wait()
     spread(qin, (), stage.at[0])
-    for step in range(STEPS):
-        spread(nin, (step,), noise.at[step])
     zeros[...] = jnp.zeros_like(zeros)
 
     def place(step, kind):
@@ -226,9 +223,15 @@
         local_copy(zeros, step, kind).wait()
 
     if comm:
+        pl.semaphore_wait(barrier, count)
+        for half in (1, 0):
+            start_shift(0, half)
+        loads[1].wait()
+
         @pl.when(first_level)
         def _():
             for step in range(STEPS):
+                spread(nin, (step,), noise.at[step])
                 for half in range(2):
                     local_copy(noise.at[step, :, 8 * half : 8 * half + 8, :], step, half).start()
 
@@ -238,15 +241,14 @@
                 for step in range(STEPS):
                     local_copy(zeros, step, 2 + half).start()
 
-        pl.semaphore_wait(barrier, count)
-        for half in (1, 0):
-            start_shift(0, half)
         for half in (1, 0):
             @pl.when(first_level & neighbour(half))
             def _(half=half):
                 for step in range(STEPS):
                     noise_copy(step, half).start()
 
+    if not comm:
+        loads[1].wait()
     for half in range(2):
         for pair in range(2):
             for odd in range(2):
@@ -262,7 +264,7 @@
     lo_mask, hi_mask = (g > 0).astype(F32), not_last.astype(F32)
     for step in range(STEPS):
         now = q.at[step]
-        early = 1 - step % 2
+        early = step % 2
         late = 1 - early
 
         def send_terms(half):
@@ -302,16 +304,18 @@
         low = 2 * early
         units = [(early, 0), (early, 1), (late, 0), (late, 1)]
         fresh_rows = (0, 1) if early else (4, 5)
-        rows_of = [(low, low + 2, low + 1, low + 3)] * 2 + [fresh_rows] * 2
+        rows_of = [fresh_rows if half == late else (low, low + 2, low + 1, low + 3) for half, _ in units]
+        windowed = [early]
         first(early, 0, rows_of[0])
         shape(early, 0, 0)
         for u, (half, pair) in enumerate(units):
             for j in range(4):
-                if j == 1 and u == 1:
-                    if comm:
-                        wait_latents(step, 2 + late)
-                    window_columns(late, now, x1)
                 if j in (1, 2) and u < 3:
+                    if units[u + 1][0] not in windowed:
+                        if comm:
+                            wait_latents(step, 2 + late)
+                        window_columns(late, now, x1)
+                        windowed.append(late)
                     rows = rows_of[u + 1]
                     first(*units[u + 1], rows[: len(rows) // 2] if j == 1 else rows[len(rows) // 2 :])
                 product(half, pair, j, wt, ust, products)
@@ -321,13 +325,14 @@
                     shape(*units[u + 1], 0)
                 if j == 0 and u:
                     second_rows(*units[u - 1], products, held)
-                if j == 2 and u:
+                if j == 1 and u:
                     term_rows(*units[u - 1], pst, held, sums)
-                    if u in (1, 3):
-                        send_terms(early if u == 1 else late)
+                    if units[u - 1][1] == 0:
+                        send_terms(units[u - 1][0])
+                if u == 3 and j == 3:
+                    finish(early)
         second_rows(*units[3], products, held)
-        finish(early)
-        term_rows(late, 1, pst, held, sums)
+        term_rows(*units[3], pst, held, sums)
         finish(late)
 
     for frame in range(4):

time: 36 us -> 33.1 us (0.919)
  Pallas kernels: 34.4 us -> 31.4 us
    pallas_call x1, Pallas kernels: 34.4 us -> 31.4 us  [call(): pl.pallas_call(functools.partial(kernel, levels, tiles, comm), out_shape=...]
where the time goes in v3:
time: 33.1 us; the launch traced here: 32.7 us
  Pallas kernels  31.4 us (95%)
  local copies, waits for them, and re-layouts  1.33 us (4%)
    pallas_call x1, Pallas kernels, call(): pl.pallas_call(functools.partial(kernel, levels, tiles, comm), out_shape=...  31.4 us
    unnamed x1, local copies, waits for them, and re-layouts  1.33 us

profile of v3, /device:TPU:7, one launch (start us, length us, event | category | flops | bytes accessed | tf_op | source)
XLA Modules:
  0.0 32.7 jit_solution(18278980221357613482)
XLA Ops:
  0.0 31.4 %queue_steps.1 = bf16[4,4,4,128]{3,2,1,0:T(4,128)(2,1)} custom-call(bf16[4,4,4,128]{3,2,1,0:T(4,128)(2,1)} %bitcast.9, bf16[2,4,4,4,128]{4,3,2,1,0:T(4,128)(2,1)} %noise_hbm.1, bf16[9,4,320]{2,1,0:T(4,128)(2,1)} %bitcast.8, bf16[9,320,320]{2,1,0:T(8,128)(2,1)} %bitcast.6, bf16[3,320,320]{2,1,0:T(8,128)(2,1)} %tw_hbm.1, bf16[4,320]{1,0:T(4,128)(2,1)} %op_hbm.1, ...), custom_call_target="tpu_custom_call" | custom-call | tf_op jit(solution)/shard_map/queue_steps/pallas_call | solution.py:396
  31.4 1.3 %copy.10 = bf16[1,4,4,4,128]{4,3,2,1,0:T(4,128)(2,1)} copy(bf16[1,4,4,4,128]{4,3,2,1,0:T(4,128)(2,1)} %bitcast.7) | data formatting | bytes 32768

commit v4 on v3

--- a/solution.py
+++ b/solution.py
@@ -75,10 +75,12 @@
             pst[odd, place * 8 : place * 8 + 8, 384 : 384 + CH] = through[k][rows]
 
 
-def window_columns(half, q, x1):
+def window_columns(half, q, x1, far=None):
     for block in range(4):
         lanes = slice(block * COLS, (block + 1) * COLS)
-        if half == 0:
+        if far is not None:
+            value = jnp.concatenate([far[block], q[block, 0:16, :], jnp.zeros((8, COLS), F32)], axis=0)
+        elif half == 0:
             value = jnp.concatenate([q[block, 0:24, :], jnp.zeros((8, COLS), F32)], axis=0)
         else:
             value = jnp.concatenate([jnp.zeros((8, COLS), F32), q[block, 8:32, :]], axis=0)
@@ -110,12 +112,13 @@
     products[half, pair, j] = jnp.dot(wt[j], ust[half, pair, j], preferred_element_type=F32)
 
 
-def second_rows(half, pair, products, held):
+def second_rows(half, pair, products, held, slot=None):
+    slot = half if slot is None else slot
     for odd in range(2):
         one, two = products[half, pair, 1], products[half, pair, 2]
         value = products[half, pair, 0] + one + two if odd == 0 else one - two - products[half, pair, 3]
-        held[half, pair, odd, 0:CH, :] = value.astype(BF16)
-        held[half, pair, odd, 384 : 384 + CH, :] = (value + value * jnp.tanh(value)).astype(BF16)
+        held[slot, pair, odd, 0:CH, :] = value.astype(BF16)
+        held[slot, pair, odd, 384 : 384 + CH, :] = (value + value * jnp.tanh(value)).astype(BF16)
 
 
 def term_rows(half, pair, pst, held, sums):
@@ -134,13 +137,18 @@
 
 def kernel(levels, tiles, comm, queue_hbm, noise_hbm, cf_hbm, cs_hbm, tw_hbm, op_hbm, keep, rate, out,
            qin, nin, cf, cs, tw, op, wt, w1t, w1, p16, pst, q, stage, noise, zeros, x1, act, ust, products, held, sums,
-           lo_send, hi_send, lo_recv, hi_recv, load_sem, send_sem, recv_sem, term_send_sem, term_recv_sem):
+           lo_send, hi_send, lo_recv, hi_recv, load_sem, send_sem, recv_sem, term_send_sem, term_recv_sem,
+           far_ready, far, border, far_send_sem, far_recv_sem):
     if comm:
         g, t = lax.axis_index("level"), lax.axis_index("tile")
     else:
         g, t = jnp.int32(0), jnp.int32(1)
     has_up, has_down = t > 0, t < tiles - 1
     first_level, not_last = g == 0, g < levels - 1
+    period = max(tiles // 4, 1)
+    edge = has_up & (lax.rem(t, period) == 0)
+    next_edge = has_down & (lax.rem(t + 1, period) == 0)
+    redo, next_redo = edge, next_edge
 
     loads = [
         pltpu.make_async_copy(source, target, load_sem.at[i])
@@ -162,13 +170,14 @@
                 if dg == 0:
                     ok = ok & first_level
 
-                @pl.when(ok)
+                @pl.when(ok & jnp.logical_not(next_edge) if dt == 1 else ok)
                 def _(dg=dg, dt=dt):
                     pl.semaphore_signal(
                         barrier, inc=1, device_id=(lax.rem(g + dg + levels, levels), t + dt), device_id_type=MESH
                     )
 
-                count = count + ok.astype(jnp.int32)
+                counted = ok & jnp.logical_not(edge) if dt == -1 else ok
+                count = count + counted.astype(jnp.int32)
 
     loads[0].wait()
     spread(qin, (), stage.at[0])
@@ -207,23 +216,62 @@
             for i, (source, target, dg) in enumerate([(lo_send, hi_recv, levels - 1), (hi_send, lo_recv, 1)])
         ]
 
-    def neighbour(half):
+    def neighbour(half, step=0):
+        if half and step:
+            return has_down & jnp.logical_not(next_redo)
         return has_down if half else has_up
+
+    def far_copy(source, level, send):
+        return pltpu.make_async_remote_copy(
+            src_ref=source, dst_ref=far, send_sem=far_send_sem.at[send], recv_sem=far_recv_sem,
+            device_id=(level, t + 1), device_id_type=MESH,
+        )
+
+    def far_copies():
+        return [
+            (next_redo & not_last, far_copy(stage.at[0, :, 0:8, :], g + 1, 0)),
+            (next_redo & first_level, far_copy(noise.at[0, :, 0:8, :], 0 * g, 1)),
+        ]
+
+    def border_copy():
+        return pltpu.make_async_remote_copy(
+            src_ref=border, dst_ref=place(1, 2), send_sem=far_send_sem.at[2], recv_sem=recv_sem.at[1, 2],
+            device_id=(g + 1, t), device_id_type=MESH,
+        )
 
     def start_shift(step, half):
         @pl.when(not_last)
         def _():
             main_copy(step, half).start()
 
-            @pl.when(neighbour(half))
+            @pl.when(neighbour(half) & jnp.logical_not(edge) if step == 0 and half == 0 else neighbour(half, step))
             def _():
                 halo_copy(step, half).start()
 
+    def far_sends():
+        pl.semaphore_wait(far_ready, 2 + first_level.astype(jnp.int32))
+
+        @pl.when(not_last)
+        def _():
+            halo_copy(0, 0).start()
+
+        @pl.when(first_level)
+        def _():
+            for step in range(STEPS):
+                noise_copy(step, 0).start()
+
     def wait_latents(step, kind):
         local_copy(zeros, step, kind).wait()
 
     if comm:
         pl.semaphore_wait(barrier, count)
+        for dg in (-1, 0, 1):
+            @pl.when(next_edge & first_level if dg == 0 else next_edge)
+            def _(dg=dg):
+                pl.semaphore_signal(
+                    far_ready, inc=1, device_id=(lax.rem(g + dg + levels, levels), t + 1), device_id_type=MESH
+                )
+
         for half in (1, 0):
             start_shift(0, half)
         loads[1].wait()
@@ -242,14 +290,19 @@
                     local_copy(zeros, step, 2 + half).start()
 
         for half in (1, 0):
-            @pl.when(first_level & neighbour(half))
+            @pl.when(first_level & neighbour(half) & (jnp.logical_not(edge) if half == 0 else has_down))
             def _(half=half):
                 for step in range(STEPS):
                     noise_copy(step, half).start()
 
+        for ok, copy in far_copies():
+            @pl.when(ok)
+            def _(copy=copy):
+                copy.start()
+
     if not comm:
         loads[1].wait()
-    for half in range(2):
+    for half in range(3):
         for pair in range(2):
             for odd in range(2):
                 held[half, pair, odd, CH:384, :] = jnp.zeros((64, 256), BF16)
@@ -262,9 +315,8 @@
     prepare_second(cs, wt)
 
     lo_mask, hi_mask = (g > 0).astype(F32), not_last.astype(F32)
-    for step in range(STEPS):
+    def run(step, early, far_tile):
         now = q.at[step]
-        early = step % 2
         late = 1 - early
 
         def send_terms(half):
@@ -284,10 +336,18 @@
                 before = lo_recv[step, half] * lo_mask if frame == 0 else part_of(sums, half, 1, frame - 1)
                 after = hi_recv[step, half] * hi_mask if frame == 3 else part_of(sums, half, 2, frame + 1)
                 projected = part_of(sums, half, 0, frame) + before + after
-                latent = now[block, 8 + 8 * half : 16 + 8 * half, :]
+                latent = now[block, 0:8, :] if half == 2 else now[block, 8 + 8 * half : 16 + 8 * half, :]
                 fresh = keep[step, g, frame] * latent - rate[step, g, frame] * projected
-                stage[step + 1, block, rows, :] = fresh.astype(BF16).astype(F32)
-            if comm and step + 1 < STEPS:
+                fresh = fresh.astype(BF16).astype(F32)
+                if half == 2:
+                    border[block] = fresh
+                else:
+                    stage[step + 1, block, rows, :] = fresh
+            if comm and half == 2:
+                @pl.when(not_last)
+                def _():
+                    border_copy().start()
+            elif comm and step + 1 < STEPS:
                 start_shift(step + 1, half)
 
         if comm:
@@ -303,6 +363,8 @@
         window_columns(early, now, x1)
         low = 2 * early
         units = [(early, 0), (early, 1), (late, 0), (late, 1)]
+        if step == 1:
+            units = [units[0], units[2], units[1], units[3]]
         fresh_rows = (0, 1) if early else (4, 5)
         rows_of = [fresh_rows if half == late else (low, low + 2, low + 1, low + 3) for half, _ in units]
         windowed = [early]
@@ -313,6 +375,8 @@
                 if j in (1, 2) and u < 3:
                     if units[u + 1][0] not in windowed:
                         if comm:
+                            if far_tile:
+                                far_sends()
                             wait_latents(step, 2 + late)
                         window_columns(late, now, x1)
                         windowed.append(late)
@@ -335,11 +399,61 @@
         term_rows(*units[3], pst, held, sums)
         finish(late)
 
+        if far_tile:
+            if True:
+                pltpu.make_async_copy(zeros, far, far_recv_sem).wait()
+                window_columns(0, now, x1, far)
+                first(0, 0, (0, 2, 1, 3))
+                shape(0, 0, 0)
+                for pair in range(2):
+                    for j in range(4):
+                        if pair == 0 and j in (1, 2):
+                            first(0, 1, (0, 2) if j == 1 else (1, 3))
+                        product(0, pair, j, wt, ust, products)
+                        if j < 3:
+                            shape(0, pair, j + 1)
+                        elif pair == 0:
+                            shape(0, 1, 0)
+                        if pair and j == 0:
+                            second_rows(0, 0, products, held, 2)
+                        if pair and j == 1:
+                            term_rows(2, 0, pst, held, sums)
+                            send_terms(2)
+                second_rows(0, 1, products, held, 2)
+                term_rows(2, 1, pst, held, sums)
+                finish(2)
+
+    if comm:
+        @pl.when(edge)
+        def _():
+            run(0, 1, True)
+
+        @pl.when(jnp.logical_not(edge))
+        def _():
+            run(0, 0, False)
+    else:
+        run(0, 0, False)
+    run(1, 1, False)
+
     for frame in range(4):
         for channel in range(4):
             out[frame, channel] = stage[STEPS, block_of(frame), pl.ds(channel, 4, stride=4), :].astype(BF16)
 
     if comm:
+        for ok, copy in far_copies():
+            @pl.when(ok)
+            def _(copy=copy):
+                copy.wait_send()
+
+        @pl.when(redo)
+        def _():
+            for copy in term_copies(0, 2):
+                copy.wait_send()
+
+            @pl.when(not_last)
+            def _():
+                border_copy().wait_send()
+
         for step in range(STEPS):
             for half in range(2):
                 for copy in term_copies(step, half):
@@ -349,7 +463,7 @@
                 def _(step=step, half=half):
                     main_copy(step, half).wait_send()
 
-                    @pl.when(neighbour(half))
+                    @pl.when(neighbour(half, step))
                     def _():
                         halo_copy(step, half).wait_send()
 
@@ -381,17 +495,22 @@
         pltpu.VMEM((2, 6, CH, 256), BF16),
         pltpu.VMEM((2, 2, 4, 3 * CH, 256), BF16),
         pltpu.VMEM((2, 2, 4, CH, 256), F32),
-        pltpu.VMEM((2, 2, 2, 704, 256), BF16),
-        pltpu.VMEM((2, 2, 3, 8, 256), F32),
-        pltpu.VMEM((STEPS, 2, 8, COLS), F32),
-        pltpu.VMEM((STEPS, 2, 8, COLS), F32),
-        pltpu.VMEM((STEPS, 2, 8, COLS), F32),
-        pltpu.VMEM((STEPS, 2, 8, COLS), F32),
+        pltpu.VMEM((3, 2, 2, 704, 256), BF16),
+        pltpu.VMEM((3, 2, 3, 8, 256), F32),
+        pltpu.VMEM((STEPS, 3, 8, COLS), F32),
+        pltpu.VMEM((STEPS, 3, 8, COLS), F32),
+        pltpu.VMEM((STEPS, 3, 8, COLS), F32),
+        pltpu.VMEM((STEPS, 3, 8, COLS), F32),
         pltpu.SemaphoreType.DMA((6,)),
         pltpu.SemaphoreType.DMA((STEPS, 6)),
         pltpu.SemaphoreType.DMA((STEPS, 4)),
-        pltpu.SemaphoreType.DMA((STEPS, 2, 2)),
-        pltpu.SemaphoreType.DMA((STEPS, 2, 2)),
+        pltpu.SemaphoreType.DMA((STEPS, 3, 2)),
+        pltpu.SemaphoreType.DMA((STEPS, 3, 2)),
+        pltpu.SemaphoreType.REGULAR,
+        pltpu.VMEM((4, 8, COLS), F32),
+        pltpu.VMEM((4, 8, COLS), F32),
+        pltpu.SemaphoreType.DMA((3,)),
+        pltpu.SemaphoreType.DMA,
     ]
     return pl.pallas_call(
         functools.partial(kernel, levels, tiles, comm),

time: 33.1 us -> 32.3 us (0.976)
  Pallas kernels: 31.4 us -> 30.6 us
    pallas_call x1, Pallas kernels: 31.4 us -> 30.6 us  [call(): pl.pallas_call(functools.partial(kernel, levels, tiles, comm), out_shape=...]
where the time goes in v4:
time: 32.3 us; the launch traced here: 31.9 us
  Pallas kernels  30.6 us (95%)
  local copies, waits for them, and re-layouts  1.33 us (4%)
    pallas_call x1, Pallas kernels, call(): pl.pallas_call(functools.partial(kernel, levels, tiles, comm), out_shape=...  30.6 us
    unnamed x1, local copies, waits for them, and re-layouts  1.33 us

profile of v4, /device:TPU:7, one launch (start us, length us, event | category | flops | bytes accessed | tf_op | source)
XLA Modules:
  0.0 31.9 jit_solution(5354632088436709064)
XLA Ops:
  0.0 30.6 %queue_steps.1 = bf16[4,4,4,128]{3,2,1,0:T(4,128)(2,1)} custom-call(bf16[4,4,4,128]{3,2,1,0:T(4,128)(2,1)} %bitcast.9, bf16[2,4,4,4,128]{4,3,2,1,0:T(4,128)(2,1)} %noise_hbm.1, bf16[9,4,320]{2,1,0:T(4,128)(2,1)} %bitcast.8, bf16[9,320,320]{2,1,0:T(8,128)(2,1)} %bitcast.6, bf16[3,320,320]{2,1,0:T(8,128)(2,1)} %tw_hbm.1, bf16[4,320]{1,0:T(4,128)(2,1)} %op_hbm.1, ...), custom_call_target="tpu_custom_call" | custom-call | tf_op jit(solution)/shard_map/queue_steps/pallas_call | solution.py:515
  30.6 1.3 %copy.10 = bf16[1,4,4,4,128]{4,3,2,1,0:T(4,128)(2,1)} copy(bf16[1,4,4,4,128]{4,3,2,1,0:T(4,128)(2,1)} %bitcast.7) | data formatting | bytes 32768

commit v5 on v4

--- a/solution.py
+++ b/solution.py
@@ -310,7 +310,6 @@
     prepare_first(cf, w1t, w1, has_up.astype(F32), has_down.astype(F32))
     loads[3].wait()
     loads[4].wait()
-    prepare_projection(op, tw, p16, pst)
     loads[5].wait()
     prepare_second(cs, wt)
 
@@ -387,13 +386,15 @@
                     shape(half, pair, j + 1)
                 elif u < 3:
                     shape(*units[u + 1], 0)
+                if step == 0 and u == 0 and j == 3:
+                    prepare_projection(op, tw, p16, pst)
                 if j == 0 and u:
                     second_rows(*units[u - 1], products, held)
                 if j == 1 and u:
                     term_rows(*units[u - 1], pst, held, sums)
                     if units[u - 1][1] == 0:
                         send_terms(units[u - 1][0])
-                if u == 3 and j == 3:
+                if u == 3 and j == 2:
                     finish(early)
         second_rows(*units[3], products, held)
         term_rows(*units[3], pst, held, sums)

time: 32.3 us -> 32.3 us (level)
  no operation moved by 1% of the time
where the time goes in v5:
time: 32.3 us; the launch traced here: 31.9 us
  Pallas kernels  30.6 us (95%)
  local copies, waits for them, and re-layouts  1.33 us (4%)
    pallas_call x1, Pallas kernels, call(): pl.pallas_call(functools.partial(kernel, levels, tiles, comm), out_shape=...  30.6 us
    unnamed x1, local copies, waits for them, and re-layouts  1.33 us

profile of v5, /device:TPU:7, one launch (start us, length us, event | category | flops | bytes accessed | tf_op | source)
XLA Modules:
  0.0 31.9 jit_solution(14562537344525023202)
XLA Ops:
  0.0 30.6 %queue_steps.1 = bf16[4,4,4,128]{3,2,1,0:T(4,128)(2,1)} custom-call(bf16[4,4,4,128]{3,2,1,0:T(4,128)(2,1)} %bitcast.9, bf16[2,4,4,4,128]{4,3,2,1,0:T(4,128)(2,1)} %noise_hbm.1, bf16[9,4,320]{2,1,0:T(4,128)(2,1)} %bitcast.8, bf16[9,320,320]{2,1,0:T(8,128)(2,1)} %bitcast.6, bf16[3,320,320]{2,1,0:T(8,128)(2,1)} %tw_hbm.1, bf16[4,320]{1,0:T(4,128)(2,1)} %op_hbm.1, ...), custom_call_target="tpu_custom_call" | custom-call | tf_op jit(solution)/shard_map/queue_steps/pallas_call | solution.py:516
  30.6 1.3 %copy.10 = bf16[1,4,4,4,128]{4,3,2,1,0:T(4,128)(2,1)} copy(bf16[1,4,4,4,128]{4,3,2,1,0:T(4,128)(2,1)} %bitcast.7) | data formatting | bytes 32768
